TPU v7x, 512 devices: a whole 4x4x16 slice. The times are simulated.
512 devices in a mesh: section: 8 (over x, core), dp: 64 (over y, z).
Axes of the slice: x: 4, y: 4, z: 16, core: 2. Of those that a mesh axis runs over, the one named last changes fastest.
Arguments:
- stream_in: bfloat16 [128, 8192], P(None, 'dp'), may hold values from -6 to 6
- gains: float32 [8, 8192], P('section'), may hold values from 0.5 to 1.5
- weights: bfloat16 [8, 8192, 8192], P('section', 'dp'), may hold values from -6 to 6
- masks: int32 [8, 8192, 128], P('section', 'dp'), may hold values 0 or 1
- inv_hessian: float32 [8, 64, 128, 128], P('section', 'dp'), may hold values from -0.025 to 3.2
Outputs:
- stream_out: bfloat16 [8, 128, 8192], P('section', None, 'dp')
- refitted: bfloat16 [8, 8192, 8192], P('section', 'dp')
All inputs are finite; a program needn't handle non-finite values. No bound on the sum of `masks` on one device may be relied on, other than what follows from the above.
Results may differ from a plain program's by a relative error of at most 0.015.
Values may be sent and summed in bfloat16 or wider, within the bound.
No kernel may reach another device: no remote copies, remote signals or barrier semaphores. Data moves between devices by JAX's collectives and lax.ppermute only.
A program may use at most 64 MiB of HBM per device.

v0:
```python
import jax
import jax.numpy as jnp
from jax import lax
from jax.sharding import PartitionSpec as P

D = 8192
BLOCK = 128


def passed_along(value, axis, steps):
    count = lax.axis_size(axis)
    first, last = (max(0, -steps), min(count, count - steps))
    return lax.ppermute(value, axis, [(source, source + steps) for source in range(first, last)])


def body(stream_in, gains, weights, masks, inv_hessian):
    section_index = lax.axis_index("section")
    dp_index = lax.axis_index("dp")
    owned_cols = stream_in.shape[1]
    keep = jnp.repeat(masks[0], BLOCK // 2, axis=1)
    kept_rows = weights[0] * keep.astype(jnp.bfloat16)
    gain_row = gains[0]
    tok_count = stream_in.shape[0]
    micro_count = 4
    micro_rows = tok_count // micro_count
    step_count = lax.axis_size("section") + micro_count - 1
    scale = D ** (-0.5)
    inverse_whole = inv_hessian[0]

    def advance(moment, state):
        outgoing, normed_store, produced = state
        received = passed_along(outgoing, "section", 1)
        micro_index = moment - section_index
        active = (micro_index >= 0) & (micro_index < micro_count)
        offset = jnp.clip(micro_index, 0, micro_count - 1) * micro_rows
        x_rows = lax.dynamic_slice_in_dim(stream_in, offset, micro_rows, 0)
        window = jnp.where(section_index == 0, x_rows, received)
        widened = lax.all_gather(window, "dp", axis=1, tiled=True).astype(jnp.float32)
        mean_square = jnp.mean(widened * widened, axis=1, keepdims=True)
        normed = (widened * lax.rsqrt(mean_square + 1e-05) * gain_row).astype(jnp.bfloat16)
        projected = (
            lax.dot_general(
                normed, kept_rows, (((1,), (1,)), ((), ())), preferred_element_type=jnp.float32
            )
            * scale
        )
        new_window = (window.astype(jnp.float32) + projected).astype(jnp.bfloat16)
        stored = lax.dynamic_slice_in_dim(normed, dp_index * owned_cols, owned_cols, 1)
        prior_normed = lax.dynamic_slice_in_dim(normed_store, offset, micro_rows, 0)
        normed_store = lax.dynamic_update_slice_in_dim(
            normed_store, jnp.where(active, stored, prior_normed), offset, 0
        )
        prior_out = lax.dynamic_slice_in_dim(produced, offset, micro_rows, 0)
        produced = lax.dynamic_update_slice_in_dim(
            produced, jnp.where(active, new_window, prior_out), offset, 0
        )
        return (new_window, normed_store, produced)

    start_state = (
        jnp.zeros((micro_rows, owned_cols), jnp.bfloat16),
        jnp.zeros((tok_count, owned_cols), jnp.bfloat16),
        jnp.zeros((tok_count, owned_cols), jnp.bfloat16),
    )
    outgoing, normed_store, produced = lax.fori_loop(0, step_count, advance, start_state)
    blocks = normed_store.reshape(tok_count, -1, BLOCK)
    gram_local = jnp.einsum("tbi,tbj->bij", blocks, blocks, preferred_element_type=jnp.float32)
    out_rows = weights.shape[1]
    removed = weights[0].astype(jnp.float32) * (1 - keep).astype(jnp.float32)
    removed = removed.reshape(out_rows, -1, BLOCK)
    hessian_local = gram_local * (1.0 / tok_count)
    hessian, inverse = (
        lax.all_gather(hessian_local.astype(jnp.bfloat16), "dp", axis=0, tiled=True).astype(
            hessian_local.dtype
        ),
        lax.all_gather(inverse_whole.astype(jnp.bfloat16), "dp", axis=0, tiled=True).astype(
            inverse_whole.dtype
        ),
    )
    gradient = jnp.einsum("rbi,bij->rbj", removed, hessian, precision=lax.Precision.HIGHEST)
    update_step = jnp.einsum("rbi,bij->rbj", gradient, inverse, precision=lax.Precision.HIGHEST)
    refitted = keep.astype(jnp.float32) * (
        weights[0].astype(jnp.float32) + update_step.reshape(out_rows, -1)
    )
    return (produced[None], refitted.astype(jnp.bfloat16)[None])


def solution(mesh):
    placed = (
        P(None, "dp"),
        P("section", None),
        P("section", "dp", None),
        P("section", "dp", None),
        P("section", "dp", None, None),
    )
    return jax.shard_map(
        body,
        mesh=mesh,
        in_specs=placed,
        out_specs=(P("section", None, "dp"), P("section", "dp", None)),
        check_vma=False,
    )
```

profile of v0, /device:TPU:2, one launch (start us, length us, event | category | flops | bytes accessed | tf_op | source)
XLA Modules:
  0.0 1489.9 jit_solution(13567906170957561185)
XLA Ops:
  7.2 3.3 copy.17
  16.3 1178.1 %while.20 = (s32[]{:T(128)}, bf16[32,128]{1,0:T(8,128)(2,1)S(1)}, bf16[128,128]{1,0:T(8,128)(2,1)S(1)}, bf16[128,128]{1,0:T(8,128)(2,1)S(1)}, pred[]{:T(512)}, /...) while((s32[]{:T(128)}, bf16[32,128]{1,0:T(8,128)(2,1)S(1)}, ...), condition=%wide.region_2.3_spmd.clone, body=%wide.region_0.2_spmd.clone.sunk | while | flops 68976688 | bytes 4891457 | solution.py:64
  22.0 108.0 %all_gather.19 = bf16[32,8192]{1,0:T(8,128)(2,1)S(1)} all-gather(bf16[32,128]{1,0:T(8,128)(2,1)S(1)} %dynamic-slice_select_fusion.2), channel_id=1, replica_groups=mesh['section'=8,'dp'=64] {'dp'}, dimensions={1}, use_global_device_ids=true | all-gather | bytes 532480 | tf_op jit(solution)/shard_map/while/body/eval_jaxpr/all_gather | solution.py:38
  133.2 3.0 collective-permute-done
  137.0 99.8 %all_gather.19 = bf16[32,8192]{1,0:T(8,128)(2,1)S(1)} all-gather(bf16[32,128]{1,0:T(8,128)(2,1)S(1)} %dynamic-slice_select_fusion.2), channel_id=1, replica_groups=mesh['section'=8,'dp'=64] {'dp'}, dimensions={1}, use_global_device_ids=true | all-gather | bytes 532480 | tf_op jit(solution)/shard_map/while/body/eval_jaxpr/all_gather | solution.py:38
  240.0 3.0 collective-permute-done
  243.8 98.8 %all_gather.19 = bf16[32,8192]{1,0:T(8,128)(2,1)S(1)} all-gather(bf16[32,128]{1,0:T(8,128)(2,1)S(1)} %dynamic-slice_select_fusion.2), channel_id=1, replica_groups=mesh['section'=8,'dp'=64] {'dp'}, dimensions={1}, use_global_device_ids=true | all-gather | bytes 532480 | tf_op jit(solution)/shard_map/while/body/eval_jaxpr/all_gather | solution.py:38
  349.6 99.8 %all_gather.19 = bf16[32,8192]{1,0:T(8,128)(2,1)S(1)} all-gather(bf16[32,128]{1,0:T(8,128)(2,1)S(1)} %dynamic-slice_select_fusion.2), channel_id=1, replica_groups=mesh['section'=8,'dp'=64] {'dp'}, dimensions={1}, use_global_device_ids=true | all-gather | bytes 532480 | tf_op jit(solution)/shard_map/while/body/eval_jaxpr/all_gather | solution.py:38
  452.7 3.0 collective-permute-done
  456.4 98.8 %all_gather.19 = bf16[32,8192]{1,0:T(8,128)(2,1)S(1)} all-gather(bf16[32,128]{1,0:T(8,128)(2,1)S(1)} %dynamic-slice_select_fusion.2), channel_id=1, replica_groups=mesh['section'=8,'dp'=64] {'dp'}, dimensions={1}, use_global_device_ids=true | all-gather | bytes 532480 | tf_op jit(solution)/shard_map/while/body/eval_jaxpr/all_gather | solution.py:38
  558.5 3.0 collective-permute-done
  562.2 99.8 %all_gather.19 = bf16[32,8192]{1,0:T(8,128)(2,1)S(1)} all-gather(bf16[32,128]{1,0:T(8,128)(2,1)S(1)} %dynamic-slice_select_fusion.2), channel_id=1, replica_groups=mesh['section'=8,'dp'=64] {'dp'}, dimensions={1}, use_global_device_ids=true | all-gather | bytes 532480 | tf_op jit(solution)/shard_map/while/body/eval_jaxpr/all_gather | solution.py:38
  665.3 3.0 collective-permute-done
  669.0 98.8 %all_gather.19 = bf16[32,8192]{1,0:T(8,128)(2,1)S(1)} all-gather(bf16[32,128]{1,0:T(8,128)(2,1)S(1)} %dynamic-slice_select_fusion.2), channel_id=1, replica_groups=mesh['section'=8,'dp'=64] {'dp'}, dimensions={1}, use_global_device_ids=true | all-gather | bytes 532480 | tf_op jit(solution)/shard_map/while/body/eval_jaxpr/all_gather | solution.py:38
  771.1 3.0 collective-permute-done
  774.8 99.8 %all_gather.19 = bf16[32,8192]{1,0:T(8,128)(2,1)S(1)} all-gather(bf16[32,128]{1,0:T(8,128)(2,1)S(1)} %dynamic-slice_select_fusion.2), channel_id=1, replica_groups=mesh['section'=8,'dp'=64] {'dp'}, dimensions={1}, use_global_device_ids=true | all-gather | bytes 532480 | tf_op jit(solution)/shard_map/while/body/eval_jaxpr/all_gather | solution.py:38
  881.6 98.7 %all_gather.19 = bf16[32,8192]{1,0:T(8,128)(2,1)S(1)} all-gather(bf16[32,128]{1,0:T(8,128)(2,1)S(1)} %dynamic-slice_select_fusion.2), channel_id=1, replica_groups=mesh['section'=8,'dp'=64] {'dp'}, dimensions={1}, use_global_device_ids=true | all-gather | bytes 532480 | tf_op jit(solution)/shard_map/while/body/eval_jaxpr/all_gather | solution.py:38
  987.4 99.7 %all_gather.19 = bf16[32,8192]{1,0:T(8,128)(2,1)S(1)} all-gather(bf16[32,128]{1,0:T(8,128)(2,1)S(1)} %dynamic-slice_select_fusion.2), channel_id=1, replica_groups=mesh['section'=8,'dp'=64] {'dp'}, dimensions={1}, use_global_device_ids=true | all-gather | bytes 532480 | tf_op jit(solution)/shard_map/while/body/eval_jaxpr/all_gather | solution.py:38
  1094.2 98.9 %all_gather.19 = bf16[32,8192]{1,0:T(8,128)(2,1)S(1)} all-gather(bf16[32,128]{1,0:T(8,128)(2,1)S(1)} %dynamic-slice_select_fusion.2), channel_id=1, replica_groups=mesh['section'=8,'dp'=64] {'dp'}, dimensions={1}, use_global_device_ids=true | all-gather | bytes 532480 | tf_op jit(solution)/shard_map/while/body/eval_jaxpr/all_gather | solution.py:38
  1200.4 130.9 %all-gather.5.cloned.1.call-done = bf16[8192,128]{1,0:T(8,128)(2,1)} async-done(((bf16[128,128]{1,0:T(8,128)(2,1)}), bf16[8192,128]{1,0:T(8,128)(2,1)}) %all-gather.5.cloned.1.call-update) | async-done | bytes 2097168 | tf_op jit(solution)/shard_map/all_gather | solution.py:72
  1331.4 7.5 fusion.9
  1338.8 132.5 %all-gather.7.cloned.1.call-done = bf16[64,1,128,128]{3,2,1,0:T(8,128)(2,1)} async-done(((bf16[1,1,128,128]{3,2,1,0:T(8,128)(2,1)}), bf16[64,1,128,128]{3,2,1,0:T(8,128)(2,1)}) %all-gather.7.cloned.1.call-update) | async-done | bytes 2097168 | tf_op jit(solution)/shard_map/all_gather | solution.py:75
  1471.3 5.8 fusion.5
  1479.0 4.1 copy.27
  (123 shorter events, 72.0 us)
Async XLA Ops:
  7.2 1324.2 %all-gather.5.cloned.1.call-start = ((), (), s32[]{:S(2)}) async-start(), calls=%async_computation | async-start | bytes 2129920 | tf_op jit(solution)/shard_map/all_gather | solution.py:72
  7.2 3.3 copy-start.4
  10.5 1.3 copy-start
  13.3 3.0 copy-start.2
  16.3 1179.0 %copy-start.5 = (f32[1,1,128,128]{3,2,1,0:T(8,128)S(1)}, f32[1,1,128,128]{3,2,1,0:T(8,128)}, u32[]{:S(2)}) copy-start(f32[1,1,128,128]{3,2,1,0:T(8,128)} %param.11) | copy-start | bytes 196612
  16.3 5.0 collective-permute-start
  131.3 5.0 collective-permute-start
  238.1 5.0 collective-permute-start
  343.9 5.0 collective-permute-start
  450.7 5.0 collective-permute-start
  556.5 5.0 collective-permute-start
  663.3 5.0 collective-permute-start
  769.1 5.0 collective-permute-start
  876.0 5.0 collective-permute-start
  981.7 5.0 collective-permute-start
  1088.5 5.0 collective-permute-start
  1194.4 2.1 copy-start.3
  1195.2 276.1 %all-gather.7.cloned.1.call-start = ((), (), s32[]{:S(2)}) async-start(), calls=%async_computation.1 | async-start | bytes 2129920 | tf_op jit(solution)/shard_map/all_gather | solution.py:75
  1196.1 1.6 copy-start.1
Sparse Core Ops, SparseCore 0:
  1195.3 135.9 all-gather.4
  1334.3 136.9 all-gather.6
where the time goes:
time: 1490 us
  blocking collectives  1100 us (74%)
  waiting for transfers between devices  297 us (20%)
  matrix products  23.4 us (2%)
  starting transfers between devices  21.2 us (1%)
  other arithmetic  19.6 us (1%)
    all_gather x11, blocking collectives, advance(): lax.all_gather(window, 'dp', axis=1, tiled=True).astype(jnp.float32)  1100 us
    all_gather x1, waiting for transfers between devices, body(): lax.all_gather(inverse_whole.astype(jnp.bfloat16), 'dp', axis=0, tiled=True)  132 us
    all_gather x1, waiting for transfers between devices, body(): lax.all_gather(hessian_local.astype(jnp.bfloat16), 'dp', axis=0, tiled=True)  131 us
    ppermute x11, waiting for transfers between devices, passed_along(): lax.ppermute(value, axis, [(source, source + steps) for source in range(f...  33.3 us
  transfers between devices with their start and end apart: 13, of which 13 were waited for; matrix products, arithmetic and copies ran while one was open for 1% of the time, Pallas kernels for 0%

commit v1 on v0

v1 whole, which is shorter than its diff:
```python
import functools

import jax
import jax.numpy as jnp
from jax import lax
from jax.experimental import pallas as pl
from jax.experimental.pallas import tpu as pltpu
from jax.sharding import PartitionSpec as P

D = 8192
BLOCK = 128
HALF = BLOCK // 2
ROWS = 128
TOKENS = 128
Y = 4
Z = 16
SECTIONS = 8
SPAN = Z * BLOCK
SCALE = D ** (-0.5)
EPS = 1e-05
AXES = ("section", "dp")
Y_GROUPS = [[y * Z + z for y in range(Y)] for z in range(Z)]
Z_GROUPS = [[y * Z + z for z in range(Z)] for y in range(Y)]
BF = jnp.bfloat16
F32 = jnp.float32
NT = (((1,), (1,)), ((), ()))
TN = (((0,), (0,)), ((), ()))


def spread(masks, first, width):
    column = lax.broadcasted_iota(jnp.int32, (masks.shape[1], width), 1) + first
    row = lax.broadcasted_iota(jnp.int32, (masks.shape[1], width), 0)
    low = row * HALF
    chosen = ((column >= low) & (column < low + HALF)).astype(F32).astype(BF)
    return jnp.dot(masks.astype(F32).astype(BF), chosen, preferred_element_type=F32)


def keep_kernel(weights_ref, masks_ref, kept_ref):
    width = weights_ref.shape[1]
    keep = spread(masks_ref[...], pl.program_id(0) * width, width)
    kept_ref[0] = (weights_ref[...].astype(F32) * keep).astype(BF)


def keep_weights(weights, masks):
    return pl.pallas_call(
        keep_kernel,
        grid=(Y,),
        in_specs=[
            pl.BlockSpec((ROWS, SPAN), lambda i: (0, i)),
            pl.BlockSpec((ROWS, masks.shape[1]), lambda i: (0, 0)),
        ],
        out_specs=pl.BlockSpec((1, ROWS, SPAN), lambda i: (i, 0, 0)),
        out_shape=jax.ShapeDtypeStruct((Y, ROWS, SPAN), BF),
        name="keep_weights",
    )(weights, masks)


def layer_kernel(x_ref, own_ref, gain_ref, kept_ref, *refs):
    outs, scaled = refs[:Y], refs[Y]
    squares = jnp.zeros((TOKENS, BLOCK), F32)
    for j in range(Z):
        x = x_ref[j].astype(F32)
        squares = squares + x * x
        scaled[:, j * BLOCK : (j + 1) * BLOCK] = (
            x * gain_ref[:, j * BLOCK : (j + 1) * BLOCK]
        ).astype(BF)
    total = jnp.sum(squares, axis=1, keepdims=True)
    high = total.astype(BF)
    low = (total - high.astype(F32)).astype(BF)
    lane = lax.broadcasted_iota(jnp.int32, (TOKENS, BLOCK), 1)
    both = jnp.where(
        lane < HALF,
        jnp.broadcast_to(high.astype(F32), (TOKENS, BLOCK)),
        jnp.broadcast_to(low.astype(F32), (TOKENS, BLOCK)),
    ).astype(BF)
    partial = lax.dot_general(scaled[...], kept_ref[...], NT, preferred_element_type=F32)
    for k in range(Y):
        outs[k][:, :BLOCK] = (partial[:, k * BLOCK : (k + 1) * BLOCK] * SCALE).astype(BF)
        outs[k][:, BLOCK : 2 * BLOCK] = both
    outs[0][:, 2 * BLOCK :] = own_ref[...]


def layer(x, own, gain, kept):
    widths = [3 * BLOCK] + [2 * BLOCK] * (Y - 1)
    return pl.pallas_call(
        layer_kernel,
        out_shape=[jax.ShapeDtypeStruct((TOKENS, w), BF) for w in widths],
        scratch_shapes=[pltpu.VMEM((TOKENS, SPAN), BF)],
        name="layer",
    )(x, own, gain, kept)


def join(parts):
    projected = sum(p[:, :BLOCK].astype(F32) for p in parts)
    total = sum(
        p[:, BLOCK : BLOCK + 1].astype(F32) + p[:, BLOCK + HALF : BLOCK + HALF + 1].astype(F32)
        for p in parts
    )
    inverse = lax.rsqrt(total * (1.0 / D) + EPS)
    return (parts[0][:, 2 * BLOCK :].astype(F32) + projected * inverse).astype(BF)


PER_STEP = 8
WIDTH = PER_STEP * BLOCK


def refit_kernel(x_ref, own_ref, gain_ref, weights_ref, masks_ref, inverse_ref, stream_ref, refit_ref, norm, acc):
    step = pl.program_id(0)

    @pl.when(step == 0)
    def _():
        def add(b, squares):
            x = x_ref[b].astype(F32)
            return squares + x * x

        squares = lax.fori_loop(0, D // BLOCK, add, jnp.zeros((TOKENS, BLOCK), F32), unroll=8)
        total = jnp.sum(squares, axis=1, keepdims=True)
        norm[...] = jnp.broadcast_to(lax.rsqrt(total * (1.0 / D) + EPS), (TOKENS, BLOCK))
        acc[...] = jnp.zeros((TOKENS, ROWS), F32)

    keep = spread(masks_ref[...], step * WIDTH, WIDTH)
    scale = norm[...]
    projected = acc[...]
    for j in range(PER_STEP):
        cut = slice(j * BLOCK, (j + 1) * BLOCK)
        x = x_ref[step * PER_STEP + j].astype(F32)
        normed = (x * scale * gain_ref[:, cut]).astype(BF)
        gram = lax.dot_general(normed, normed, TN, preferred_element_type=F32)
        hessian = (gram * (1.0 / TOKENS)).astype(BF)
        product = jnp.dot(hessian, inverse_ref[j], preferred_element_type=F32).astype(BF)
        weights = weights_ref[:, cut].astype(F32)
        kept = weights * keep[:, cut]
        removed = (weights - kept).astype(BF)
        update = jnp.dot(removed, product, preferred_element_type=F32)
        refit_ref[:, cut] = (keep[:, cut] * (weights + update)).astype(BF)
        projected = projected + lax.dot_general(
            normed, kept.astype(BF), NT, preferred_element_type=F32
        )
    acc[...] = projected

    @pl.when(step == D // WIDTH - 1)
    def _():
        stream_ref[...] = (own_ref[...].astype(F32) + projected * SCALE).astype(BF)


def refit(x, own, gain, weights, masks, inverse):
    whole = lambda *shape: pl.BlockSpec(shape, lambda i: (0,) * len(shape))
    return pl.pallas_call(
        refit_kernel,
        grid=(D // WIDTH,),
        in_specs=[
            whole(D // BLOCK, TOKENS, BLOCK),
            whole(TOKENS, BLOCK),
            pl.BlockSpec((1, WIDTH), lambda i: (0, i)),
            pl.BlockSpec((ROWS, WIDTH), lambda i: (0, i)),
            whole(ROWS, masks.shape[1]),
            pl.BlockSpec((PER_STEP, BLOCK, BLOCK), lambda i: (i, 0, 0)),
        ],
        out_specs=[whole(TOKENS, ROWS), pl.BlockSpec((ROWS, WIDTH), lambda i: (0, i))],
        out_shape=[
            jax.ShapeDtypeStruct((TOKENS, ROWS), BF),
            jax.ShapeDtypeStruct((ROWS, D), BF),
        ],
        scratch_shapes=[pltpu.VMEM((TOKENS, BLOCK), F32), pltpu.VMEM((TOKENS, ROWS), F32)],
        name="refit",
    )(x, own, gain, weights, masks, inverse)


def to_next(section, shift):
    return [
        (section * Y * Z + y * Z + z, (section + 1) * Y * Z + ((y + shift) % Y) * Z + z)
        for y in range(Y)
        for z in range(Z)
    ]


def body(stream_in, gains, weights, masks, inv_hessian):
    section = lax.axis_index("section")
    y = lax.axis_index("dp") // Z
    rows = weights[0]
    mask_rows = masks[0]
    inverse = lax.all_gather(inv_hessian[0].astype(BF), "dp", axis=0, tiled=True)

    kept = keep_weights(rows, mask_rows)
    kept = lax.all_to_all(kept, "dp", 0, 0, axis_index_groups=Y_GROUPS)
    kept = lax.dynamic_slice_in_dim(jnp.concatenate([kept, kept], axis=0), y, Y, 0)
    kept = kept.reshape(Y * ROWS, SPAN)
    gain = lax.dynamic_slice_in_dim(gains, y * SPAN, SPAN, 1)

    own = stream_in
    mine = jnp.zeros((Z, TOKENS, BLOCK), BF)
    my_own = own
    for phase in range(SECTIONS):
        spread_own = jnp.broadcast_to(own[None], (Z, TOKENS, BLOCK))
        x = lax.all_to_all(spread_own, "dp", 0, 0, axis_index_groups=Z_GROUPS)
        here = section == phase
        mine = jnp.where(here, x, mine)
        my_own = jnp.where(here, own, my_own)
        if phase == SECTIONS - 1:
            break
        messages = layer(x, own, gain, kept)
        own = join(
            [lax.ppermute(m, AXES, to_next(phase, k)) for k, m in enumerate(messages)]
        )

    mine = jnp.broadcast_to(mine[None], (Y, Z, TOKENS, BLOCK))
    x = lax.all_to_all(mine, "dp", 0, 0, axis_index_groups=Y_GROUPS)
    x = x.reshape(Y * Z, TOKENS, BLOCK)
    stream, refitted = refit(x, my_own, gains, rows, mask_rows, inverse)
    return (stream[None], refitted[None])


def solution(mesh):
    placed = (
        P(None, "dp"),
        P("section", None),
        P("section", "dp", None),
        P("section", "dp", None),
        P("section", "dp", None, None),
    )
    return jax.shard_map(
        body,
        mesh=mesh,
        in_specs=placed,
        out_specs=(P("section", None, "dp"), P("section", "dp", None)),
        check_vma=False,
    )
```

time: 1490 us -> 531 us (0.36)
  blocking collectives: 1100 us -> 237 us
  waiting for transfers between devices: 297 us -> 164 us
  Pallas kernels: 0 us -> 48.1 us
  starting transfers between devices: 21.2 us -> 50.1 us
  matrix products: 23.4 us -> 0 us
    all_gather x11 -> x0, blocking collectives: 1100 us -> none  [advance(): lax.all_gather(window, 'dp', axis=1, tiled=True).astype(jnp.float32)]
    all_to_all x0 -> x7, blocking collectives: none -> 237 us  [the longest x6 206 us: body(): x = lax.all_to_all(spread_own, 'dp', 0, 0, axis_index_groups=Z_GROUPS)]
    all_gather x2 -> x1, waiting for transfers between devices: 263 us -> 98.8 us  [body(): lax.all_gather(inv_hessian[0].astype(BF), 'dp', axis=0, tiled=True)]
    all_to_all x0 -> x3, waiting for transfers between devices: none -> 53.7 us  [the longest x2 53.7 us: body(): x = lax.all_to_all(spread_own, 'dp', 0, 0, axis_index_groups=Z_GROUPS)]
    pallas_call x0 -> x9, Pallas kernels: none -> 48.1 us  [the longest x7 23.6 us: layer(): pl.pallas_call(layer_kernel, out_shape=[jax.ShapeDtypeStruct((TOKENS, w),...]
    all_to_all x0 -> x3, starting transfers between devices: none -> 25.2 us  [the longest x2 21.6 us: body(): x = lax.all_to_all(spread_own, 'dp', 0, 0, axis_index_groups=Z_GROUPS)]
    dot_general x14 -> x0, matrix products: 23.4 us -> none  [the longest x11 9.26 us: advance(): lax.dot_general(normed, kept_rows, (((1,), (1,)), ((), ())), preferred_el...]
    ppermute x11 -> x28, waiting for transfers between devices: 33.3 us -> 11.8 us  [body(): lax.ppermute(m, AXES, to_next(phase, k))]
  transfers between devices with their start and end apart: 13 -> 32, of which waited for: 13 -> 7; matrix products, arithmetic and copies ran while one was open for 1% -> 2% of each run, Pallas kernels for 0% -> 0%
where the time goes in v1:
time: 531 us; the launch traced here: 530 us
  blocking collectives  237 us (45%)
  waiting for transfers between devices  164 us (31%)
  starting transfers between devices  50.1 us (9%)
  Pallas kernels  48.1 us (9%)
  between operations  14.8 us (3%)
  other arithmetic  7.96 us (1%)
  local copies, waits for them, and re-layouts  7.77 us (1%)
    all_to_all x6, blocking collectives, body(): x = lax.all_to_all(spread_own, 'dp', 0, 0, axis_index_groups=Z_GROUPS)  206 us
    all_gather x1, waiting for transfers between devices, body(): lax.all_gather(inv_hessian[0].astype(BF), 'dp', axis=0, tiled=True)  98.8 us
    all_to_all x2, waiting for transfers between devices, body(): x = lax.all_to_all(spread_own, 'dp', 0, 0, axis_index_groups=Z_GROUPS)  53.7 us
    all_to_all x1, blocking collectives, body(): kept = lax.all_to_all(kept, 'dp', 0, 0, axis_index_groups=Y_GROUPS)  30.9 us
    ppermute x28, starting transfers between devices, body(): lax.ppermute(m, AXES, to_next(phase, k))  24.8 us
    pallas_call x7, Pallas kernels, layer(): pl.pallas_call(layer_kernel, out_shape=[jax.ShapeDtypeStruct((TOKENS, w),...  23.6 us
    all_to_all x2, starting transfers between devices, body(): x = lax.all_to_all(spread_own, 'dp', 0, 0, axis_index_groups=Z_GROUPS)  21.6 us
    pallas_call x1, Pallas kernels, refit(): pl.pallas_call(refit_kernel, grid=(D // WIDTH,), in_specs=[whole(D // BLO...  20.2 us
  transfers between devices with their start and end apart: 32, of which 7 were waited for; matrix products, arithmetic and copies ran while one was open for 2% of the time, Pallas kernels for 0%

profile of v1, /device:TPU:2, one launch (start us, length us, event | category | flops | bytes accessed | tf_op | source)
XLA Modules:
  0.0 529.6 jit_solution(17119629668840559187)
XLA Ops:
  7.2 4.4 keep_weights.1
  11.5 30.9 %all_to_all.50 = bf16[4,128,2048]{2,1,0:T(8,128)(2,1)S(1)} all-to-all(bf16[4,128,2048]{2,1,0:T(8,128)(2,1)} %keep_weights.1), channel_id=1, replica_groups={{0,16,32,48},{1,17,33,49},{2,18,34,50},{3,19,35,51},{4,20,36,52},{5,21,..., dimensions={0} | all-to-all | bytes 4194304 | tf_op jit(solution)/shard_map/all_to_all | solution.py:185
  43.4 15.2 %all-to-all-start = ((bf16[16,128,128]{2,1,0:T(8,128)(2,1)}), bf16[16,128,128]{2,1,0:T(8,128)(2,1)S(1)}, u32[]{:S(2)}, u32[]{:S(2)}) async-start(bf16[16,128,128]{2,1,0:T(8,128)(2,1)} %broadcast_in_dim.24), calls=%async_computation | async-start | bytes 1048576 | tf_op jit(solution)/shard_map/all_to_all | solution.py:195
  59.9 2.1 fusion
  62.0 23.9 %all-to-all-done.x_ref = bf16[16,128,128]{2,1,0:T(8,128)(2,1)S(1)} async-done(((bf16[16,128,128]{2,1,0:T(8,128)(2,1)}), bf16[16,128,128]{2,1,0:T(8,128)(2,1)S(1)}, u32[]{:S(2)}, u32[]{:S(2)}) %all-to-all-start) | async-done | bytes 524320 | tf_op jit(solution)/shard_map/all_to_all | solution.py:195
  86.7 3.4 layer.7
  93.2 35.1 %all_to_all.51.x_ref = bf16[16,128,128]{2,1,0:T(8,128)(2,1)} all-to-all(bf16[16,128,128]{2,1,0:T(8,128)(2,1)S(1)} %broadcast_in_dim.25), channel_id=1, replica_groups={{0,1,2,3,4,5,6,7,8,9,10,11,12,13,14,15},{16,17,18,19,20,21,22,23,24,25,..., dimensions={0} | all-to-all | bytes 1048576 | tf_op jit(solution)/shard_map/all_to_all | solution.py:195
  128.3 3.4 layer.8
  136.8 7.9 %collective-permute-done.5 = bf16[128,256]{1,0:T(8,128)(2,1)S(1)} collective-permute-done((bf16[128,256]{1,0:T(8,128)(2,1)}, bf16[128,256]{1,0:T(8,128)(2,1)S(1)}, u32[]{:S(2)}, u32[]{:S(2)}) %collective-permute-start.5) | collective-permute-done | bytes 65568 | tf_op jit(solution)/shard_map/ppermute | solution.py:203
  146.8 25.7 %all_to_all.52.x_ref = bf16[16,128,128]{2,1,0:T(8,128)(2,1)} all-to-all(bf16[16,128,128]{2,1,0:T(8,128)(2,1)S(1)} %broadcast_in_dim.26), channel_id=1, replica_groups={{0,1,2,3,4,5,6,7,8,9,10,11,12,13,14,15},{16,17,18,19,20,21,22,23,24,25,..., dimensions={0} | all-to-all | bytes 1048576 | tf_op jit(solution)/shard_map/all_to_all | solution.py:195
  172.5 3.4 layer.9
  183.6 32.4 %all_to_all.53.x_ref = bf16[16,128,128]{2,1,0:T(8,128)(2,1)} all-to-all(bf16[16,128,128]{2,1,0:T(8,128)(2,1)S(1)} %broadcast_in_dim.27), channel_id=1, replica_groups={{0,1,2,3,4,5,6,7,8,9,10,11,12,13,14,15},{16,17,18,19,20,21,22,23,24,25,..., dimensions={0} | all-to-all | bytes 1048576 | tf_op jit(solution)/shard_map/all_to_all | solution.py:195
  216.0 3.3 layer.10
  222.5 34.2 %all_to_all.54.x_ref = bf16[16,128,128]{2,1,0:T(8,128)(2,1)} all-to-all(bf16[16,128,128]{2,1,0:T(8,128)(2,1)S(1)} %broadcast_in_dim.28), channel_id=1, replica_groups={{0,1,2,3,4,5,6,7,8,9,10,11,12,13,14,15},{16,17,18,19,20,21,22,23,24,25,..., dimensions={0} | all-to-all | bytes 1048576 | tf_op jit(solution)/shard_map/all_to_all | solution.py:195
  256.7 3.4 layer.11
  263.2 41.9 %all_to_all.55.x_ref = bf16[16,128,128]{2,1,0:T(8,128)(2,1)} all-to-all(bf16[16,128,128]{2,1,0:T(8,128)(2,1)S(1)} %broadcast_in_dim.29), channel_id=1, replica_groups={{0,1,2,3,4,5,6,7,8,9,10,11,12,13,14,15},{16,17,18,19,20,21,22,23,24,25,..., dimensions={0} | all-to-all | bytes 1048576 | tf_op jit(solution)/shard_map/all_to_all | solution.py:195
  305.0 3.3 layer.12
  311.6 36.4 %all_to_all.56.x_ref = bf16[16,128,128]{2,1,0:T(8,128)(2,1)} all-to-all(bf16[16,128,128]{2,1,0:T(8,128)(2,1)S(1)} %broadcast_in_dim.30), channel_id=1, replica_groups={{0,1,2,3,4,5,6,7,8,9,10,11,12,13,14,15},{16,17,18,19,20,21,22,23,24,25,..., dimensions={0} | all-to-all | bytes 1048576 | tf_op jit(solution)/shard_map/all_to_all | solution.py:195
  348.0 3.5 layer.13
  360.4 6.4 %all-to-all-start.8 = ((bf16[16,128,128]{2,1,0:T(8,128)(2,1)}), bf16[16,128,128]{2,1,0:T(8,128)(2,1)}, u32[]{:S(2)}, u32[]{:S(2)}) async-start(bf16[16,128,128]{2,1,0:T(8,128)(2,1)} %broadcast_in_dim.31), calls=%async_computation.8 | async-start | bytes 1048576 | tf_op jit(solution)/shard_map/all_to_all | solution.py:195
  366.9 29.8 %all-to-all-done.8 = bf16[16,128,128]{2,1,0:T(8,128)(2,1)} async-done(((bf16[16,128,128]{2,1,0:T(8,128)(2,1)}), bf16[16,128,128]{2,1,0:T(8,128)(2,1)}, u32[]{:S(2)}, u32[]{:S(2)}) %all-to-all-start.8) | async-done | bytes 524320 | tf_op jit(solution)/shard_map/all_to_all | solution.py:195
  398.8 3.6 all-to-all-start.9
  402.4 98.8 %all-gather.3.cloned.1.call-done = bf16[64,1,128,128]{3,2,1,0:T(8,128)(2,1)} async-done(((bf16[1,1,128,128]{3,2,1,0:T(8,128)(2,1)}), bf16[64,1,128,128]{3,2,1,0:T(8,128)(2,1)}) %all-gather.3.cloned.1.call-update) | async-done | bytes 2097168 | tf_op jit(solution)/shard_map/all_gather | solution.py:182
  502.5 20.2 %refit.1 = (bf16[128,128]{1,0:T(8,128)(2,1)}, bf16[128,8192]{1,0:T(8,128)(2,1)}) custom-call(bf16[64,128,128]{2,1,0:T(8,128)(2,1)} %bitcast.16, bf16[128,128]{1,0:T(8,128)(2,1)} %get-tuple-element.62.own_ref, f32[1,8192]{1,0:T(1,128)} %gain_ref.1, bf16[128,8192]{1,0:T(8,128)(2,1)} %bitcast.15, s32[128,128]{1,0:T(8,128)} %bitcast.19, ...), custom_call_target="tpu_custom_call" | custom-call | tf_op jit(solution)/shard_map/refit/pallas_call | solution.py:148
  (126 shorter events, 42.4 us)
Async XLA Ops:
  43.4 42.6 %all-to-all-start = ((bf16[16,128,128]{2,1,0:T(8,128)(2,1)}), bf16[16,128,128]{2,1,0:T(8,128)(2,1)S(1)}, u32[]{:S(2)}, u32[]{:S(2)}) async-start(bf16[16,128,128]{2,1,0:T(8,128)(2,1)} %broadcast_in_dim.24), calls=%async_computation | async-start | bytes 1048576 | tf_op jit(solution)/shard_map/all_to_all | solution.py:195
  58.6 442.7 %all-gather.3.cloned.1.call-start = ((), (), s32[]{:S(2)}) async-start(), calls=%async_computation.10 | async-start | bytes 2129920 | tf_op jit(solution)/shard_map/all_gather | solution.py:182
  90.1 2.7 collective-permute-start
  90.7 2.0 collective-permute-start.1
  131.6 14.8 %collective-permute-start.4 = (bf16[128,384]{1,0:T(8,128)(2,1)}, bf16[128,384]{1,0:T(8,128)(2,1)S(1)}, u32[]{:S(2)}, u32[]{:S(2)}) collective-permute-start(bf16[128,384]{1,0:T(8,128)(2,1)} %get-tuple-element.36), channel_id=1, source_target_pairs={{64,128},{65,129},{66,130},{67,131},{68,132},{69,133},{70,134},{71... | collective-permute-start | bytes 294920 | tf_op jit(solution)/shard_map/ppermute | solution.py:203
  132.9 11.8 %collective-permute-start.5 = (bf16[128,256]{1,0:T(8,128)(2,1)}, bf16[128,256]{1,0:T(8,128)(2,1)S(1)}, u32[]{:S(2)}, u32[]{:S(2)}) collective-permute-start(bf16[128,256]{1,0:T(8,128)(2,1)} %get-tuple-element.37), channel_id=1, source_target_pairs={{64,144},{65,145},{66,146},{67,147},{68,148},{69,149},{70,150},{71... | collective-permute-start | bytes 196616 | tf_op jit(solution)/shard_map/ppermute | solution.py:203
  134.2 12.2 %collective-permute-start.6 = (bf16[128,256]{1,0:T(8,128)(2,1)}, bf16[128,256]{1,0:T(8,128)(2,1)S(1)}, u32[]{:S(2)}, u32[]{:S(2)}) collective-permute-start(bf16[128,256]{1,0:T(8,128)(2,1)} %get-tuple-element.38), channel_id=1, source_target_pairs={{64,160},{65,161},{66,162},{67,163},{68,164},{69,165},{70,166},{71... | collective-permute-start | bytes 196616 | tf_op jit(solution)/shard_map/ppermute | solution.py:203
  135.5 10.9 %collective-permute-start.7 = (bf16[128,256]{1,0:T(8,128)(2,1)}, bf16[128,256]{1,0:T(8,128)(2,1)S(1)}, u32[]{:S(2)}, u32[]{:S(2)}) collective-permute-start(bf16[128,256]{1,0:T(8,128)(2,1)} %get-tuple-element.39), channel_id=1, source_target_pairs={{64,176},{65,177},{66,178},{67,179},{68,180},{69,181},{70,182},{71... | collective-permute-start | bytes 196616 | tf_op jit(solution)/shard_map/ppermute | solution.py:203
  175.8 7.4 %collective-permute-start.8 = (bf16[128,384]{1,0:T(8,128)(2,1)}, bf16[128,384]{1,0:T(8,128)(2,1)S(1)}, u32[]{:S(2)}, u32[]{:S(2)}) collective-permute-start(bf16[128,384]{1,0:T(8,128)(2,1)} %get-tuple-element.40), channel_id=1, source_target_pairs={{128,192},{129,193},{130,194},{131,195},{132,196},{133,197},{134,1... | collective-permute-start | bytes 294920 | tf_op jit(solution)/shard_map/ppermute | solution.py:203
  177.1 3.9 collective-permute-start.10
  178.4 3.5 collective-permute-start.11
  179.7 3.5 collective-permute-start.9
  219.4 2.7 collective-permute-start.12
  220.0 2.0 collective-permute-start.13
  260.0 2.7 collective-permute-start.16
  260.7 2.0 collective-permute-start.17
  308.4 2.7 collective-permute-start.20
  309.0 2.0 collective-permute-start.21
  351.5 5.4 %collective-permute-start.24 = (bf16[128,384]{1,0:T(8,128)(2,1)}, bf16[128,384]{1,0:T(8,128)(2,1)S(1)}, u32[]{:S(2)}, u32[]{:S(2)}) collective-permute-start(bf16[128,384]{1,0:T(8,128)(2,1)} %get-tuple-element.56), channel_id=1, source_target_pairs={{384,448},{385,449},{386,450},{387,451},{388,452},{389,453},{390,4... | collective-permute-start | bytes 294920 | tf_op jit(solution)/shard_map/ppermute | solution.py:203
  352.2 4.7 collective-permute-start.25
  352.9 4.1 collective-permute-start.26
  354.1 2.8 collective-permute-start.27
  360.4 36.2 %all-to-all-start.8 = ((bf16[16,128,128]{2,1,0:T(8,128)(2,1)}), bf16[16,128,128]{2,1,0:T(8,128)(2,1)}, u32[]{:S(2)}, u32[]{:S(2)}) async-start(bf16[16,128,128]{2,1,0:T(8,128)(2,1)} %broadcast_in_dim.31), calls=%async_computation.8 | async-start | bytes 1048576 | tf_op jit(solution)/shard_map/all_to_all | solution.py:195
  398.8 102.4 %all-to-all-start.9 = ((bf16[4,16,128,128]{3,2,1,0:T(8,128)(2,1)}), bf16[4,16,128,128]{3,2,1,0:T(8,128)(2,1)S(1)}, u32[]{:S(2)}, u32[]{:S(2)}) async-start(bf16[4,16,128,128]{3,2,1,0:T(8,128)(2,1)} %broadcast_in_dim.33), calls=%async_computation.9 | async-start | bytes 4194304 | tf_op jit(solution)/shard_map/all_to_all | solution.py:207
  (29 other events, 818.6 us)
Sparse Core Ops, SparseCore 0:
  357.0 144.1 all-gather.2

commit v2 on v1

--- a/solution.py
+++ b/solution.py
@@ -25,6 +25,7 @@
 F32 = jnp.float32
 NT = (((1,), (1,)), ((), ()))
 TN = (((0,), (0,)), ((), ()))
+SMALL = pltpu.CompilerParams(vmem_limit_bytes=24 << 20)
 
 
 def spread(masks, first, width):
@@ -35,28 +36,32 @@
     return jnp.dot(masks.astype(F32).astype(BF), chosen, preferred_element_type=F32)
 
 
-def keep_kernel(weights_ref, masks_ref, kept_ref):
+def keep_kernel(place_ref, weights_ref, masks_ref, kept_ref):
     width = weights_ref.shape[1]
-    keep = spread(masks_ref[...], pl.program_id(0) * width, width)
-    kept_ref[0] = (weights_ref[...].astype(F32) * keep).astype(BF)
-
-
-def keep_weights(weights, masks):
+    keep = spread(masks_ref[...], place_ref[0] * width, width)
+    kept_ref[...] = (weights_ref[...].astype(F32) * keep).astype(BF)
+
+
+def keep_weights(place, weights, masks):
     return pl.pallas_call(
         keep_kernel,
-        grid=(Y,),
-        in_specs=[
-            pl.BlockSpec((ROWS, SPAN), lambda i: (0, i)),
-            pl.BlockSpec((ROWS, masks.shape[1]), lambda i: (0, 0)),
-        ],
-        out_specs=pl.BlockSpec((1, ROWS, SPAN), lambda i: (i, 0, 0)),
-        out_shape=jax.ShapeDtypeStruct((Y, ROWS, SPAN), BF),
+        grid_spec=pltpu.PrefetchScalarGridSpec(
+            num_scalar_prefetch=1,
+            grid=(1,),
+            in_specs=[
+                pl.BlockSpec((ROWS, SPAN), lambda i, place: (0, place[0])),
+                pl.BlockSpec((ROWS, masks.shape[1]), lambda i, place: (0, 0)),
+            ],
+            out_specs=pl.BlockSpec((ROWS, SPAN), lambda i, place: (0, 0)),
+        ),
+        out_shape=jax.ShapeDtypeStruct((ROWS, SPAN), BF),
+        compiler_params=SMALL,
         name="keep_weights",
-    )(weights, masks)
-
-
-def layer_kernel(x_ref, own_ref, gain_ref, kept_ref, *refs):
-    outs, scaled = refs[:Y], refs[Y]
+    )(place.reshape(1), weights, masks)
+
+
+def layer_kernel(x_ref, own_ref, gain_ref, *refs):
+    kept_refs, outs, scaled = refs[:Y], refs[Y : 2 * Y], refs[2 * Y]
     squares = jnp.zeros((TOKENS, BLOCK), F32)
     for j in range(Z):
         x = x_ref[j].astype(F32)
@@ -73,9 +78,11 @@
         jnp.broadcast_to(high.astype(F32), (TOKENS, BLOCK)),
         jnp.broadcast_to(low.astype(F32), (TOKENS, BLOCK)),
     ).astype(BF)
-    partial = lax.dot_general(scaled[...], kept_ref[...], NT, preferred_element_type=F32)
     for k in range(Y):
-        outs[k][:, :BLOCK] = (partial[:, k * BLOCK : (k + 1) * BLOCK] * SCALE).astype(BF)
+        partial = lax.dot_general(
+            scaled[...], kept_refs[k][...], NT, preferred_element_type=F32
+        )
+        outs[k][:, :BLOCK] = (partial * SCALE).astype(BF)
         outs[k][:, BLOCK : 2 * BLOCK] = both
     outs[0][:, 2 * BLOCK :] = own_ref[...]
 
@@ -86,8 +93,9 @@
         layer_kernel,
         out_shape=[jax.ShapeDtypeStruct((TOKENS, w), BF) for w in widths],
         scratch_shapes=[pltpu.VMEM((TOKENS, SPAN), BF)],
+        compiler_params=SMALL,
         name="layer",
-    )(x, own, gain, kept)
+    )(x, own, gain, *kept)
 
 
 def join(parts):
@@ -162,6 +170,7 @@
             jax.ShapeDtypeStruct((ROWS, D), BF),
         ],
         scratch_shapes=[pltpu.VMEM((TOKENS, BLOCK), F32), pltpu.VMEM((TOKENS, ROWS), F32)],
+        compiler_params=SMALL,
         name="refit",
     )(x, own, gain, weights, masks, inverse)
 
@@ -174,38 +183,77 @@
     ]
 
 
+def along_y(shift):
+    return [
+        (s * Y * Z + y * Z + z, s * Y * Z + ((y + shift) % Y) * Z + z)
+        for s in range(SECTIONS)
+        for y in range(Y)
+        for z in range(Z)
+    ]
+
+
 def body(stream_in, gains, weights, masks, inv_hessian):
     section = lax.axis_index("section")
     y = lax.axis_index("dp") // Z
     rows = weights[0]
     mask_rows = masks[0]
-    inverse = lax.all_gather(inv_hessian[0].astype(BF), "dp", axis=0, tiled=True)
-
-    kept = keep_weights(rows, mask_rows)
-    kept = lax.all_to_all(kept, "dp", 0, 0, axis_index_groups=Y_GROUPS)
-    kept = lax.dynamic_slice_in_dim(jnp.concatenate([kept, kept], axis=0), y, Y, 0)
-    kept = kept.reshape(Y * ROWS, SPAN)
+    inverse_own = inv_hessian[0, 0].astype(BF)
+
+    def gather_y(blocks):
+        copies = jnp.broadcast_to(blocks[None], (Y,) + blocks.shape)
+        got = lax.all_to_all(copies, "dp", 0, 0, axis_index_groups=Y_GROUPS)
+        return got.reshape((Y * Z,) + blocks.shape[1:])
+
+    def gather_z(own):
+        copies = jnp.broadcast_to(own[None], (Z, TOKENS, BLOCK))
+        return lax.all_to_all(copies, "dp", 0, 0, axis_index_groups=Z_GROUPS)
+
+    kept = [keep_weights(lax.rem(y + k, Y), rows, mask_rows) for k in range(Y)]
+    kept = [kept[0]] + [
+        lax.ppermute(kept[Y - k], AXES, along_y(Y - k)) for k in range(1, Y)
+    ]
     gain = lax.dynamic_slice_in_dim(gains, y * SPAN, SPAN, 1)
 
     own = stream_in
-    mine = jnp.zeros((Z, TOKENS, BLOCK), BF)
+    mine = lax.cond(
+        section != 1,
+        gather_z,
+        lambda o: jnp.zeros((Z, TOKENS, BLOCK), BF),
+        jnp.where(section == 0, own, inverse_own),
+    )
+    inverse_z = mine
     my_own = own
-    for phase in range(SECTIONS):
-        spread_own = jnp.broadcast_to(own[None], (Z, TOKENS, BLOCK))
-        x = lax.all_to_all(spread_own, "dp", 0, 0, axis_index_groups=Z_GROUPS)
+    inverse = jnp.zeros((Y * Z, BLOCK, BLOCK), BF)
+    widths = [3 * BLOCK] + [2 * BLOCK] * (Y - 1)
+    for phase in range(SECTIONS - 1):
         here = section == phase
-        mine = jnp.where(here, x, mine)
+
+        def active(mine, own, *kept):
+            x = gather_z(own) if phase else mine
+            return [x, *layer(x, own, gain, kept)]
+
+        def idle(mine, own, *kept):
+            return [mine] + [jnp.zeros((TOKENS, w), BF) for w in widths]
+
+        mine, *messages = lax.cond(here, active, idle, mine, own, *kept)
         my_own = jnp.where(here, own, my_own)
-        if phase == SECTIONS - 1:
-            break
-        messages = layer(x, own, gain, kept)
-        own = join(
-            [lax.ppermute(m, AXES, to_next(phase, k)) for k, m in enumerate(messages)]
-        )
-
-    mine = jnp.broadcast_to(mine[None], (Y, Z, TOKENS, BLOCK))
-    x = lax.all_to_all(mine, "dp", 0, 0, axis_index_groups=Y_GROUPS)
-    x = x.reshape(Y * Z, TOKENS, BLOCK)
+        parts = [lax.ppermute(m, AXES, to_next(phase, k)) for k, m in enumerate(messages)]
+        if phase == 0:
+            messages, inverse_z = lax.optimization_barrier((messages, inverse_z))
+            inverse = lax.cond(section >= 2, lambda z, i: gather_y(z), lambda z, i: i, inverse_z, inverse)
+            parts, inverse = lax.optimization_barrier((parts, inverse))
+        if phase == 2:
+            messages, inverse_own = lax.optimization_barrier((messages, inverse_own))
+            inverse = lax.cond(
+                section < 2, lambda b, i: gather_y(gather_z(b)), lambda b, i: i, inverse_own, inverse
+            )
+            parts, inverse = lax.optimization_barrier((parts, inverse))
+        own = join(parts)
+
+    last = section == SECTIONS - 1
+    mine = lax.cond(last, lambda m, o: gather_z(o), lambda m, o: m, mine, own)
+    my_own = jnp.where(last, own, my_own)
+    x = gather_y(mine)
     stream, refitted = refit(x, my_own, gains, rows, mask_rows, inverse)
     return (stream[None], refitted[None])
 

time: 531 us -> 351 us (0.66)
  the two profiles are of different devices: /device:TPU:2 before, /device:TPU:39 now
where the time goes in v2:
time: 351 us; the launch traced here: 350 us
  waiting for transfers between devices  183 us (52%)
  blocking collectives  106 us (30%)
  starting transfers between devices  30.8 us (9%)
  Pallas kernels  21.3 us (6%)
  local copies, waits for them, and re-layouts  6.03 us (2%)
    ppermute x28, waiting for transfers between devices, body(): lax.ppermute(m, AXES, to_next(phase, k))  183 us
    all_to_all x2, blocking collectives, gather_z(): return lax.all_to_all(copies, 'dp', 0, 0, axis_index_groups=Z_GROUPS)  63.4 us
    all_to_all x2, blocking collectives, gather_y(): got = lax.all_to_all(copies, 'dp', 0, 0, axis_index_groups=Y_GROUPS)  42.3 us
    ppermute x28, starting transfers between devices, body(): lax.ppermute(m, AXES, to_next(phase, k))  21.1 us
    pallas_call x1, Pallas kernels, refit(): pl.pallas_call(refit_kernel, grid=(D // WIDTH,), in_specs=[whole(D // BLO...  18.4 us
    ppermute x3, starting transfers between devices, body(): lax.ppermute(kept[Y - k], AXES, along_y(Y - k))  9.62 us
  transfers between devices with their start and end apart: 31, of which 3 were waited for; matrix products, arithmetic and copies ran while one was open for 0% of the time, Pallas kernels for 1%

profile of v2, /device:TPU:39, one launch (start us, length us, event | category | flops | bytes accessed | tf_op | source)
XLA Modules:
  0.0 350.2 jit_solution(11137118820976304289)
XLA Ops:
  0.7 1.6 copy-done
  2.2 0.8 copy-done.2
  3.4 4.8 %collective-permute-start = (bf16[128,2048]{1,0:T(8,128)(2,1)S(1)}, bf16[128,2048]{1,0:T(8,128)(2,1)}, u32[]{:S(2)}, u32[]{:S(2)}) collective-permute-start(bf16[128,2048]{1,0:T(8,128)(2,1)S(1)} %keep_weights.5), channel_id=1, source_target_pairs={{0,48},{1,49},{2,50},{3,51},{4,52},{5,53},{6,54},{7,55},{8,56},{9,... | collective-permute-start | bytes 1572872 | tf_op jit(solution)/shard_map/ppermute | solution.py:213
  8.6 2.3 collective-permute-start.1
  10.9 1.1 keep_weights.7
  12.0 2.6 collective-permute-start.2
  14.6 1.1 keep_weights.4
  15.7 39.1 %conditional.11 = (bf16[16,128,128]{2,1,0:T(8,128)(2,1)}) conditional(s32[]{:T(128)} %convert_element_type.343, () %tuple.91, (pred[]{:T(512)}, bf16[128,128]{1,0:T(8,128)(2,1)S(1)}, bf16[128,128]{1,0:T(8,128)(2,1)S(1)}) %tuple.138), branch_computations={%region_0.1_spmd, %region_1.2_spmd} | conditional | flops 16384 | bytes 1703945 | solution.py:218
  15.9 39.0 %all_to_all.49 = bf16[16,128,128]{2,1,0:T(8,128)(2,1)} all-to-all(bf16[16,128,128]{2,1,0:T(8,128)(2,1)S(1)} %broadcast_in_dim.20), channel_id=1, replica_groups={{0,1,2,3,4,5,6,7,8,9,10,11,12,13,14,15},{16,17,18,19,20,21,22,23,24,25,..., dimensions={0} | all-to-all | bytes 1048576 | tf_op jit(solution)/shard_map/cond/branch_1_fun/all_to_all | solution.py:209
  57.7 25.3 %conditional.13 = (bf16[64,128,128]{2,1,0:T(8,128)(2,1)}) conditional(s32[]{:T(128)} %convert_element_type.347, () %tuple.94, bf16[16,128,128]{2,1,0:T(8,128)(2,1)} %get-tuple-element.349), branch_computations={%region_4.5_spmd, %region_5.6_spmd} | conditional | bytes 6815752 | solution.py:243
  57.7 1.6 broadcast_in_dim.34
  59.3 23.7 %all_to_all.50 = bf16[4,16,128,128]{3,2,1,0:T(8,128)(2,1)} all-to-all(bf16[4,16,128,128]{3,2,1,0:T(8,128)(2,1)S(1)} %broadcast_in_dim.34), channel_id=1, replica_groups={{0,16,32,48},{1,17,33,49},{2,18,34,50},{3,19,35,51},{4,20,36,52},{5,21,..., dimensions={0} | all-to-all | bytes 4194304 | tf_op jit(solution)/shard_map/cond/branch_1_fun/all_to_all | solution.py:204
  99.0 1.3 collective-permute-start.27
  100.3 1.3 collective-permute-start.28
  101.6 1.3 collective-permute-start.29
  102.9 1.3 collective-permute-start.30
  104.2 180.9 %collective-permute-done.28 = bf16[128,256]{1,0:T(8,128)(2,1)S(1)} collective-permute-done((bf16[128,256]{1,0:T(8,128)(2,1)S(1)}, bf16[128,256]{1,0:T(8,128)(2,1)S(1)}, u32[]{:S(2)}, u32[]{:S(2)}) %collective-permute-start.28) | collective-permute-done | bytes 65568 | tf_op jit(solution)/shard_map/ppermute | solution.py:240
  285.1 0.9 collective-permute-done.29
  286.0 0.8 collective-permute-done.30
  287.1 24.5 %conditional.21 = (bf16[16,128,128]{2,1,0:T(8,128)(2,1)}) conditional(s32[]{:T(128)} %convert_element_type.336, bf16[16,128,128]{2,1,0:T(8,128)(2,1)} %get-tuple-element.267, bf16[128,128]{1,0:T(8,128)(2,1)S(1)} %get-tuple-element.280), branch_computations={%region_20.21_spmd, %region_21.22_spmd} | conditional | bytes 1605640 | solution.py:254
  287.2 24.4 %all_to_all.59 = bf16[16,128,128]{2,1,0:T(8,128)(2,1)} all-to-all(bf16[16,128,128]{2,1,0:T(8,128)(2,1)S(1)} %broadcast_in_dim.51), channel_id=1, replica_groups={{0,1,2,3,4,5,6,7,8,9,10,11,12,13,14,15},{16,17,18,19,20,21,22,23,24,25,..., dimensions={0} | all-to-all | bytes 1048576 | tf_op jit(solution)/shard_map/cond/branch_1_fun/all_to_all | solution.py:209
  311.6 1.5 broadcast_in_dim.59
  313.2 18.7 %all_to_all.60 = bf16[4,16,128,128]{3,2,1,0:T(8,128)(2,1)S(1)} all-to-all(bf16[4,16,128,128]{3,2,1,0:T(8,128)(2,1)S(1)} %broadcast_in_dim.59), channel_id=1, replica_groups={{0,16,32,48},{1,17,33,49},{2,18,34,50},{3,19,35,51},{4,20,36,52},{5,21,..., dimensions={0} | all-to-all | bytes 4194304 | tf_op jit(solution)/shard_map/all_to_all | solution.py:204
  331.8 18.4 %refit.1 = (bf16[128,128]{1,0:T(8,128)(2,1)}, bf16[128,8192]{1,0:T(8,128)(2,1)}) custom-call(bf16[64,128,128]{2,1,0:T(8,128)(2,1)S(1)} %bitcast.18, bf16[128,128]{1,0:T(8,128)(2,1)S(1)} %get-tuple-element.279.own_ref, f32[1,8192]{1,0:T(1,128)S(1)} %copy-done.4, bf16[128,8192]{1,0:T(8,128)(2,1)S(1)} %bitcast.17, s32[128,128]{1,0:T(8,128)S(1)} %bitcast.23, ...), custom_call_target="tpu_custom_call" | custom-call | tf_op jit(solution)/shard_map/refit/pallas_call | solution.py:156
  (125 shorter events, 19.8 us)
Async XLA Ops:
  3.4 51.5 %collective-permute-start = (bf16[128,2048]{1,0:T(8,128)(2,1)S(1)}, bf16[128,2048]{1,0:T(8,128)(2,1)}, u32[]{:S(2)}, u32[]{:S(2)}) collective-permute-start(bf16[128,2048]{1,0:T(8,128)(2,1)S(1)} %keep_weights.5), channel_id=1, source_target_pairs={{0,48},{1,49},{2,50},{3,51},{4,52},{5,53},{6,54},{7,55},{8,56},{9,... | collective-permute-start | bytes 1572872 | tf_op jit(solution)/shard_map/ppermute | solution.py:213
  8.6 46.4 %collective-permute-start.1 = (bf16[128,2048]{1,0:T(8,128)(2,1)S(1)}, bf16[128,2048]{1,0:T(8,128)(2,1)}, u32[]{:S(2)}, u32[]{:S(2)}) collective-permute-start(bf16[128,2048]{1,0:T(8,128)(2,1)S(1)} %keep_weights.6), channel_id=1, source_target_pairs={{0,32},{1,33},{2,34},{3,35},{4,36},{5,37},{6,38},{7,39},{8,40},{9,... | collective-permute-start | bytes 1572872 | tf_op jit(solution)/shard_map/ppermute | solution.py:213
  12.0 42.9 %collective-permute-start.2 = (bf16[128,2048]{1,0:T(8,128)(2,1)}, bf16[128,2048]{1,0:T(8,128)(2,1)}, u32[]{:S(2)}, u32[]{:S(2)}) collective-permute-start(bf16[128,2048]{1,0:T(8,128)(2,1)} %keep_weights.7), channel_id=1, source_target_pairs={{0,16},{1,17},{2,18},{3,19},{4,20},{5,21},{6,22},{7,23},{8,24},{9,... | collective-permute-start | bytes 1572872 | tf_op jit(solution)/shard_map/ppermute | solution.py:213
  55.0 28.0 %collective-permute-start.3 = (bf16[128,384]{1,0:T(8,128)(2,1)S(1)}, bf16[128,384]{1,0:T(8,128)(2,1)S(1)}, u32[]{:S(2)}, u32[]{:S(2)}) collective-permute-start(bf16[128,384]{1,0:T(8,128)(2,1)S(1)} %get-tuple-element.227), channel_id=1, source_target_pairs={{0,64},{1,65},{2,66},{3,67},{4,68},{5,69},{6,70},{7,71},{8,72},{9,... | collective-permute-start | bytes 294920 | tf_op jit(solution)/shard_map/ppermute | solution.py:240
  55.7 27.3 %collective-permute-start.4 = (bf16[128,256]{1,0:T(8,128)(2,1)S(1)}, bf16[128,256]{1,0:T(8,128)(2,1)S(1)}, u32[]{:S(2)}, u32[]{:S(2)}) collective-permute-start(bf16[128,256]{1,0:T(8,128)(2,1)S(1)} %get-tuple-element.228), channel_id=1, source_target_pairs={{0,80},{1,81},{2,82},{3,83},{4,84},{5,85},{6,86},{7,87},{8,88},{9,... | collective-permute-start | bytes 196616 | tf_op jit(solution)/shard_map/ppermute | solution.py:240
  56.4 26.7 %collective-permute-start.5 = (bf16[128,256]{1,0:T(8,128)(2,1)S(1)}, bf16[128,256]{1,0:T(8,128)(2,1)S(1)}, u32[]{:S(2)}, u32[]{:S(2)}) collective-permute-start(bf16[128,256]{1,0:T(8,128)(2,1)S(1)} %get-tuple-element.229), channel_id=1, source_target_pairs={{0,96},{1,97},{2,98},{3,99},{4,100},{5,101},{6,102},{7,103},{8,104... | collective-permute-start | bytes 196616 | tf_op jit(solution)/shard_map/ppermute | solution.py:240
  57.0 26.0 %collective-permute-start.6 = (bf16[128,256]{1,0:T(8,128)(2,1)S(1)}, bf16[128,256]{1,0:T(8,128)(2,1)S(1)}, u32[]{:S(2)}, u32[]{:S(2)}) collective-permute-start(bf16[128,256]{1,0:T(8,128)(2,1)S(1)} %get-tuple-element.230), channel_id=1, source_target_pairs={{0,112},{1,113},{2,114},{3,115},{4,116},{5,117},{6,118},{7,119},{8... | collective-permute-start | bytes 196616 | tf_op jit(solution)/shard_map/ppermute | solution.py:240
  83.4 2.7 collective-permute-start.7
  84.1 2.0 collective-permute-start.10
  84.8 1.4 collective-permute-start.8
  86.5 2.7 collective-permute-start.11
  87.2 2.0 collective-permute-start.12
  87.9 1.4 collective-permute-start.13
  89.7 2.7 collective-permute-start.15
  90.4 2.0 collective-permute-start.16
  91.0 1.4 collective-permute-start.17
  92.8 2.7 collective-permute-start.19
  93.5 2.0 collective-permute-start.20
  95.9 2.7 collective-permute-start.23
  96.6 2.0 collective-permute-start.24
  99.0 187.8 %collective-permute-start.27 = (bf16[128,384]{1,0:T(8,128)(2,1)S(1)}, bf16[128,384]{1,0:T(8,128)(2,1)S(1)}, u32[]{:S(2)}, u32[]{:S(2)}) collective-permute-start(bf16[128,384]{1,0:T(8,128)(2,1)S(1)} %get-tuple-element.268), channel_id=1, source_target_pairs={{384,448},{385,449},{386,450},{387,451},{388,452},{389,453},{390,4... | collective-permute-start | bytes 294920 | tf_op jit(solution)/shard_map/ppermute | solution.py:240
  100.3 184.8 %collective-permute-start.28 = (bf16[128,256]{1,0:T(8,128)(2,1)S(1)}, bf16[128,256]{1,0:T(8,128)(2,1)S(1)}, u32[]{:S(2)}, u32[]{:S(2)}) collective-permute-start(bf16[128,256]{1,0:T(8,128)(2,1)S(1)} %get-tuple-element.269), channel_id=1, source_target_pairs={{384,464},{385,465},{386,466},{387,467},{388,468},{389,469},{390,4... | collective-permute-start | bytes 196616 | tf_op jit(solution)/shard_map/ppermute | solution.py:240
  101.6 184.4 %collective-permute-start.29 = (bf16[128,256]{1,0:T(8,128)(2,1)S(1)}, bf16[128,256]{1,0:T(8,128)(2,1)S(1)}, u32[]{:S(2)}, u32[]{:S(2)}) collective-permute-start(bf16[128,256]{1,0:T(8,128)(2,1)S(1)} %get-tuple-element.270), channel_id=1, source_target_pairs={{384,480},{385,481},{386,482},{387,483},{388,484},{389,485},{390,4... | collective-permute-start | bytes 196616 | tf_op jit(solution)/shard_map/ppermute | solution.py:240
  102.9 183.9 %collective-permute-start.30 = (bf16[128,256]{1,0:T(8,128)(2,1)S(1)}, bf16[128,256]{1,0:T(8,128)(2,1)S(1)}, u32[]{:S(2)}, u32[]{:S(2)}) collective-permute-start(bf16[128,256]{1,0:T(8,128)(2,1)S(1)} %get-tuple-element.271), channel_id=1, source_target_pairs={{384,496},{385,497},{386,498},{387,499},{388,500},{389,501},{390,5... | collective-permute-start | bytes 196616 | tf_op jit(solution)/shard_map/ppermute | solution.py:240
  (16 other events, 113.3 us)

commit v3 on v2

--- a/solution.py
+++ b/solution.py
@@ -108,11 +108,31 @@
     return (parts[0][:, 2 * BLOCK :].astype(F32) + projected * inverse).astype(BF)
 
 
-PER_STEP = 8
+def mask_kernel(masks_ref, keep_ref):
+    width = keep_ref.shape[1]
+    keep_ref[...] = spread(masks_ref[...], pl.program_id(0) * width, width).astype(BF)
+
+
+def spread_masks(masks):
+    return pl.pallas_call(
+        mask_kernel,
+        grid=(Y,),
+        in_specs=[pl.BlockSpec((ROWS, masks.shape[1]), lambda i: (0, 0))],
+        out_specs=pl.BlockSpec((ROWS, SPAN), lambda i: (0, i)),
+        out_shape=jax.ShapeDtypeStruct((ROWS, D), BF),
+        compiler_params=SMALL,
+        name="spread_masks",
+    )(masks)
+
+
+PER_STEP = 16
 WIDTH = PER_STEP * BLOCK
 
 
-def refit_kernel(x_ref, own_ref, gain_ref, weights_ref, masks_ref, inverse_ref, stream_ref, refit_ref, norm, acc):
+def refit_kernel(
+    x_ref, own_ref, gain_ref, weights_ref, keep_ref, inverse_ref, stream_ref, refit_ref,
+    norm, acc, normed, met, turned,
+):
     step = pl.program_id(0)
 
     @pl.when(step == 0)
@@ -126,53 +146,59 @@
         norm[...] = jnp.broadcast_to(lax.rsqrt(total * (1.0 / D) + EPS), (TOKENS, BLOCK))
         acc[...] = jnp.zeros((TOKENS, ROWS), F32)
 
-    keep = spread(masks_ref[...], step * WIDTH, WIDTH)
     scale = norm[...]
-    projected = acc[...]
-    for j in range(PER_STEP):
-        cut = slice(j * BLOCK, (j + 1) * BLOCK)
+    cuts = [slice(j * BLOCK, (j + 1) * BLOCK) for j in range(PER_STEP)]
+    for j, cut in enumerate(cuts):
         x = x_ref[step * PER_STEP + j].astype(F32)
-        normed = (x * scale * gain_ref[:, cut]).astype(BF)
-        gram = lax.dot_general(normed, normed, TN, preferred_element_type=F32)
-        hessian = (gram * (1.0 / TOKENS)).astype(BF)
-        product = jnp.dot(hessian, inverse_ref[j], preferred_element_type=F32).astype(BF)
-        weights = weights_ref[:, cut].astype(F32)
-        kept = weights * keep[:, cut]
-        removed = (weights - kept).astype(BF)
-        update = jnp.dot(removed, product, preferred_element_type=F32)
-        refit_ref[:, cut] = (keep[:, cut] * (weights + update)).astype(BF)
-        projected = projected + lax.dot_general(
-            normed, kept.astype(BF), NT, preferred_element_type=F32
+        normed[:, cut] = (x * scale * gain_ref[:, cut]).astype(BF)
+    weights = weights_ref[...]
+    keep = keep_ref[...]
+    kept = weights * keep
+    removed = weights - kept
+    acc[...] += lax.dot_general(normed[...], kept, NT, preferred_element_type=F32)
+    for j, cut in enumerate(cuts):
+        product = lax.dot_general(
+            removed[:, cut], normed[:, cut], NT, preferred_element_type=F32
         )
-    acc[...] = projected
+        met[:, cut] = (product * (1.0 / TOKENS)).astype(BF)
+        turned[:, cut] = jnp.dot(
+            normed[:, cut], inverse_ref[j], preferred_element_type=F32
+        ).astype(BF)
+    for cut in cuts:
+        update = jnp.dot(met[:, cut], turned[:, cut], preferred_element_type=F32)
+        refit_ref[:, cut] = (
+            keep[:, cut].astype(F32) * (weights[:, cut].astype(F32) + update)
+        ).astype(BF)
 
     @pl.when(step == D // WIDTH - 1)
     def _():
-        stream_ref[...] = (own_ref[...].astype(F32) + projected * SCALE).astype(BF)
-
-
-def refit(x, own, gain, weights, masks, inverse):
+        stream_ref[...] = (own_ref[...].astype(F32) + acc[...] * SCALE).astype(BF)
+
+
+def refit(x, own, gain, weights, keep, inverse):
     whole = lambda *shape: pl.BlockSpec(shape, lambda i: (0,) * len(shape))
+    cut = lambda rows: pl.BlockSpec((rows, WIDTH), lambda i: (0, i))
     return pl.pallas_call(
         refit_kernel,
         grid=(D // WIDTH,),
         in_specs=[
             whole(D // BLOCK, TOKENS, BLOCK),
             whole(TOKENS, BLOCK),
-            pl.BlockSpec((1, WIDTH), lambda i: (0, i)),
-            pl.BlockSpec((ROWS, WIDTH), lambda i: (0, i)),
-            whole(ROWS, masks.shape[1]),
+            cut(1),
+            cut(ROWS),
+            cut(ROWS),
             pl.BlockSpec((PER_STEP, BLOCK, BLOCK), lambda i: (i, 0, 0)),
         ],
-        out_specs=[whole(TOKENS, ROWS), pl.BlockSpec((ROWS, WIDTH), lambda i: (0, i))],
+        out_specs=[whole(TOKENS, ROWS), cut(ROWS)],
         out_shape=[
             jax.ShapeDtypeStruct((TOKENS, ROWS), BF),
             jax.ShapeDtypeStruct((ROWS, D), BF),
         ],
-        scratch_shapes=[pltpu.VMEM((TOKENS, BLOCK), F32), pltpu.VMEM((TOKENS, ROWS), F32)],
+        scratch_shapes=[pltpu.VMEM((TOKENS, BLOCK), F32), pltpu.VMEM((TOKENS, ROWS), F32)]
+        + [pltpu.VMEM((ROWS, WIDTH), BF)] * 3,
         compiler_params=SMALL,
         name="refit",
-    )(x, own, gain, weights, masks, inverse)
+    )(x, own, gain, weights, keep, inverse)
 
 
 def to_next(section, shift):
@@ -242,6 +268,10 @@
             messages, inverse_z = lax.optimization_barrier((messages, inverse_z))
             inverse = lax.cond(section >= 2, lambda z, i: gather_y(z), lambda z, i: i, inverse_z, inverse)
             parts, inverse = lax.optimization_barrier((parts, inverse))
+        if phase == 1:
+            messages, mask_rows = lax.optimization_barrier((messages, mask_rows))
+            keep = spread_masks(mask_rows)
+            parts, keep = lax.optimization_barrier((parts, keep))
         if phase == 2:
             messages, inverse_own = lax.optimization_barrier((messages, inverse_own))
             inverse = lax.cond(
@@ -254,7 +284,7 @@
     mine = lax.cond(last, lambda m, o: gather_z(o), lambda m, o: m, mine, own)
     my_own = jnp.where(last, own, my_own)
     x = gather_y(mine)
-    stream, refitted = refit(x, my_own, gains, rows, mask_rows, inverse)
+    stream, refitted = refit(x, my_own, gains, rows, keep, inverse)
     return (stream[None], refitted[None])
 
 

time: 351 us -> 338 us (0.963)
  Pallas kernels: 21.3 us -> 10.4 us
  waiting for transfers between devices: 183 us -> 179 us
    pallas_call x1, Pallas kernels: 18.4 us -> 6.13 us  [refit(): pl.pallas_call(refit_kernel, grid=(D // WIDTH,), in_specs=[whole(D // BLO...]
    ppermute x28, waiting for transfers between devices: 183 us -> 179 us  [body(): lax.ppermute(m, AXES, to_next(phase, k))]
  transfers between devices with their start and end apart: 31 -> 31, of which waited for: 3 -> 3; matrix products, arithmetic and copies ran while one was open for 0% -> 1% of each run, Pallas kernels for 1% -> 1%
where the time goes in v3:
time: 338 us; the launch traced here: 337 us
  waiting for transfers between devices  179 us (53%)
  blocking collectives  106 us (31%)
  starting transfers between devices  30.9 us (9%)
  Pallas kernels  10.4 us (3%)
  local copies, waits for them, and re-layouts  7.02 us (2%)
    ppermute x28, waiting for transfers between devices, body(): lax.ppermute(m, AXES, to_next(phase, k))  179 us
    all_to_all x2, blocking collectives, gather_z(): return lax.all_to_all(copies, 'dp', 0, 0, axis_index_groups=Z_GROUPS)  63.4 us
    all_to_all x2, blocking collectives, gather_y(): got = lax.all_to_all(copies, 'dp', 0, 0, axis_index_groups=Y_GROUPS)  42.5 us
    ppermute x28, starting transfers between devices, body(): lax.ppermute(m, AXES, to_next(phase, k))  21.3 us
    ppermute x3, starting transfers between devices, body(): lax.ppermute(kept[Y - k], AXES, along_y(Y - k))  9.62 us
  transfers between devices with their start and end apart: 31, of which 3 were waited for; matrix products, arithmetic and copies ran while one was open for 1% of the time, Pallas kernels for 1%

profile of v3, /device:TPU:39, one launch (start us, length us, event | category | flops | bytes accessed | tf_op | source)
XLA Modules:
  0.0 336.9 jit_solution(16190098418261222289)
XLA Ops:
  0.7 1.6 copy-done
  3.4 4.8 %collective-permute-start = (bf16[128,2048]{1,0:T(8,128)(2,1)S(1)}, bf16[128,2048]{1,0:T(8,128)(2,1)}, u32[]{:S(2)}, u32[]{:S(2)}) collective-permute-start(bf16[128,2048]{1,0:T(8,128)(2,1)S(1)} %keep_weights.5), channel_id=1, source_target_pairs={{0,48},{1,49},{2,50},{3,51},{4,52},{5,53},{6,54},{7,55},{8,56},{9,... | collective-permute-start | bytes 1572872 | tf_op jit(solution)/shard_map/ppermute | solution.py:239
  8.6 2.3 collective-permute-start.1
  10.9 1.1 keep_weights.7
  12.0 2.6 collective-permute-start.2
  14.6 1.1 keep_weights.4
  15.8 39.1 %conditional.11 = (bf16[16,128,128]{2,1,0:T(8,128)(2,1)}) conditional(s32[]{:T(128)} %convert_element_type.343, () %tuple.93, (pred[]{:T(512)}, bf16[128,128]{1,0:T(8,128)(2,1)S(1)}, bf16[128,128]{1,0:T(8,128)(2,1)S(1)}) %tuple.142), branch_computations={%region_0.1_spmd, %region_1.2_spmd} | conditional | flops 16384 | bytes 1703945 | solution.py:244
  15.9 39.0 %all_to_all.49 = bf16[16,128,128]{2,1,0:T(8,128)(2,1)} all-to-all(bf16[16,128,128]{2,1,0:T(8,128)(2,1)S(1)} %broadcast_in_dim.20), channel_id=1, replica_groups={{0,1,2,3,4,5,6,7,8,9,10,11,12,13,14,15},{16,17,18,19,20,21,22,23,24,25,..., dimensions={0} | all-to-all | bytes 1048576 | tf_op jit(solution)/shard_map/cond/branch_1_fun/all_to_all | solution.py:235
  57.7 25.3 %conditional.13 = (bf16[64,128,128]{2,1,0:T(8,128)(2,1)}) conditional(s32[]{:T(128)} %convert_element_type.347, () %tuple.96, bf16[16,128,128]{2,1,0:T(8,128)(2,1)} %get-tuple-element.361), branch_computations={%region_4.5_spmd, %region_5.6_spmd} | conditional | bytes 6815752 | solution.py:269
  57.7 1.6 broadcast_in_dim.34
  59.3 23.7 %all_to_all.50 = bf16[4,16,128,128]{3,2,1,0:T(8,128)(2,1)} all-to-all(bf16[4,16,128,128]{3,2,1,0:T(8,128)(2,1)S(1)} %broadcast_in_dim.34), channel_id=1, replica_groups={{0,16,32,48},{1,17,33,49},{2,18,34,50},{3,19,35,51},{4,20,36,52},{5,21,..., dimensions={0} | all-to-all | bytes 4194304 | tf_op jit(solution)/shard_map/cond/branch_1_fun/all_to_all | solution.py:230
  86.1 1.4 spread_masks.1.keep_ref
  87.9 1.0 copy-done.2
  101.6 1.3 collective-permute-start.27
  102.9 1.3 collective-permute-start.28
  104.2 1.3 collective-permute-start.29
  105.5 1.3 collective-permute-start.30
  106.8 177.1 %collective-permute-done.28 = bf16[128,256]{1,0:T(8,128)(2,1)S(1)} collective-permute-done((bf16[128,256]{1,0:T(8,128)(2,1)S(1)}, bf16[128,256]{1,0:T(8,128)(2,1)S(1)}, u32[]{:S(2)}, u32[]{:S(2)}) %collective-permute-start.28) | collective-permute-done | bytes 65568 | tf_op jit(solution)/shard_map/ppermute | solution.py:266
  283.9 1.6 collective-permute-done.29
  285.9 24.5 %conditional.21 = (bf16[16,128,128]{2,1,0:T(8,128)(2,1)}) conditional(s32[]{:T(128)} %convert_element_type.336, bf16[16,128,128]{2,1,0:T(8,128)(2,1)} %get-tuple-element.278, bf16[128,128]{1,0:T(8,128)(2,1)S(1)} %get-tuple-element.292), branch_computations={%region_20.21_spmd, %region_21.22_spmd} | conditional | bytes 1605640 | solution.py:284
  286.0 24.4 %all_to_all.59 = bf16[16,128,128]{2,1,0:T(8,128)(2,1)} all-to-all(bf16[16,128,128]{2,1,0:T(8,128)(2,1)S(1)} %broadcast_in_dim.51), channel_id=1, replica_groups={{0,1,2,3,4,5,6,7,8,9,10,11,12,13,14,15},{16,17,18,19,20,21,22,23,24,25,..., dimensions={0} | all-to-all | bytes 1048576 | tf_op jit(solution)/shard_map/cond/branch_1_fun/all_to_all | solution.py:235
  310.4 1.5 broadcast_in_dim.59
  312.0 18.8 %all_to_all.60 = bf16[4,16,128,128]{3,2,1,0:T(8,128)(2,1)S(1)} all-to-all(bf16[4,16,128,128]{3,2,1,0:T(8,128)(2,1)S(1)} %broadcast_in_dim.59), channel_id=1, replica_groups={{0,16,32,48},{1,17,33,49},{2,18,34,50},{3,19,35,51},{4,20,36,52},{5,21,..., dimensions={0} | all-to-all | bytes 4194304 | tf_op jit(solution)/shard_map/all_to_all | solution.py:230
  330.8 6.1 %refit.1 = (bf16[128,128]{1,0:T(8,128)(2,1)}, bf16[128,8192]{1,0:T(8,128)(2,1)}) custom-call(bf16[64,128,128]{2,1,0:T(8,128)(2,1)S(1)} %bitcast.18, bf16[128,128]{1,0:T(8,128)(2,1)S(1)} %get-tuple-element.291.own_ref, f32[1,8192]{1,0:T(1,128)S(1)} %copy-done.6, bf16[128,8192]{1,0:T(8,128)(2,1)S(1)} %bitcast.17, bf16[128,8192]{1,0:T(8,128)(2,1)S(1)} %copy-done.3, ...), custom_call_target="tpu_custom_call" | custom-call | tf_op jit(solution)/shard_map/refit/pallas_call | solution.py:181
  (130 shorter events, 20.8 us)
Async XLA Ops:
  3.4 51.5 %collective-permute-start = (bf16[128,2048]{1,0:T(8,128)(2,1)S(1)}, bf16[128,2048]{1,0:T(8,128)(2,1)}, u32[]{:S(2)}, u32[]{:S(2)}) collective-permute-start(bf16[128,2048]{1,0:T(8,128)(2,1)S(1)} %keep_weights.5), channel_id=1, source_target_pairs={{0,48},{1,49},{2,50},{3,51},{4,52},{5,53},{6,54},{7,55},{8,56},{9,... | collective-permute-start | bytes 1572872 | tf_op jit(solution)/shard_map/ppermute | solution.py:239
  8.6 46.3 %collective-permute-start.1 = (bf16[128,2048]{1,0:T(8,128)(2,1)S(1)}, bf16[128,2048]{1,0:T(8,128)(2,1)}, u32[]{:S(2)}, u32[]{:S(2)}) collective-permute-start(bf16[128,2048]{1,0:T(8,128)(2,1)S(1)} %keep_weights.6), channel_id=1, source_target_pairs={{0,32},{1,33},{2,34},{3,35},{4,36},{5,37},{6,38},{7,39},{8,40},{9,... | collective-permute-start | bytes 1572872 | tf_op jit(solution)/shard_map/ppermute | solution.py:239
  12.0 42.9 %collective-permute-start.2 = (bf16[128,2048]{1,0:T(8,128)(2,1)}, bf16[128,2048]{1,0:T(8,128)(2,1)}, u32[]{:S(2)}, u32[]{:S(2)}) collective-permute-start(bf16[128,2048]{1,0:T(8,128)(2,1)} %keep_weights.7), channel_id=1, source_target_pairs={{0,16},{1,17},{2,18},{3,19},{4,20},{5,21},{6,22},{7,23},{8,24},{9,... | collective-permute-start | bytes 1572872 | tf_op jit(solution)/shard_map/ppermute | solution.py:239
  55.0 28.0 %collective-permute-start.3 = (bf16[128,384]{1,0:T(8,128)(2,1)S(1)}, bf16[128,384]{1,0:T(8,128)(2,1)S(1)}, u32[]{:S(2)}, u32[]{:S(2)}) collective-permute-start(bf16[128,384]{1,0:T(8,128)(2,1)S(1)} %get-tuple-element.233), channel_id=1, source_target_pairs={{0,64},{1,65},{2,66},{3,67},{4,68},{5,69},{6,70},{7,71},{8,72},{9,... | collective-permute-start | bytes 294920 | tf_op jit(solution)/shard_map/ppermute | solution.py:266
  55.7 27.3 %collective-permute-start.4 = (bf16[128,256]{1,0:T(8,128)(2,1)S(1)}, bf16[128,256]{1,0:T(8,128)(2,1)S(1)}, u32[]{:S(2)}, u32[]{:S(2)}) collective-permute-start(bf16[128,256]{1,0:T(8,128)(2,1)S(1)} %get-tuple-element.234), channel_id=1, source_target_pairs={{0,80},{1,81},{2,82},{3,83},{4,84},{5,85},{6,86},{7,87},{8,88},{9,... | collective-permute-start | bytes 196616 | tf_op jit(solution)/shard_map/ppermute | solution.py:266
  56.4 26.7 %collective-permute-start.5 = (bf16[128,256]{1,0:T(8,128)(2,1)S(1)}, bf16[128,256]{1,0:T(8,128)(2,1)S(1)}, u32[]{:S(2)}, u32[]{:S(2)}) collective-permute-start(bf16[128,256]{1,0:T(8,128)(2,1)S(1)} %get-tuple-element.235), channel_id=1, source_target_pairs={{0,96},{1,97},{2,98},{3,99},{4,100},{5,101},{6,102},{7,103},{8,104... | collective-permute-start | bytes 196616 | tf_op jit(solution)/shard_map/ppermute | solution.py:266
  57.0 26.0 %collective-permute-start.6 = (bf16[128,256]{1,0:T(8,128)(2,1)S(1)}, bf16[128,256]{1,0:T(8,128)(2,1)S(1)}, u32[]{:S(2)}, u32[]{:S(2)}) collective-permute-start(bf16[128,256]{1,0:T(8,128)(2,1)S(1)} %get-tuple-element.236), channel_id=1, source_target_pairs={{0,112},{1,113},{2,114},{3,115},{4,116},{5,117},{6,118},{7,119},{8... | collective-permute-start | bytes 196616 | tf_op jit(solution)/shard_map/ppermute | solution.py:266
  83.4 4.2 %collective-permute-start.7 = (bf16[128,384]{1,0:T(8,128)(2,1)S(1)}, bf16[128,384]{1,0:T(8,128)(2,1)S(1)}, u32[]{:S(2)}, u32[]{:S(2)}) collective-permute-start(bf16[128,384]{1,0:T(8,128)(2,1)S(1)} %get-tuple-element.243), channel_id=1, source_target_pairs={{64,128},{65,129},{66,130},{67,131},{68,132},{69,133},{70,134},{71... | collective-permute-start | bytes 294920 | tf_op jit(solution)/shard_map/ppermute | solution.py:266
  84.1 3.5 %collective-permute-start.10 = (bf16[128,256]{1,0:T(8,128)(2,1)S(1)}, bf16[128,256]{1,0:T(8,128)(2,1)S(1)}, u32[]{:S(2)}, u32[]{:S(2)}) collective-permute-start(bf16[128,256]{1,0:T(8,128)(2,1)S(1)} %get-tuple-element.246), channel_id=1, source_target_pairs={{64,176},{65,177},{66,178},{67,179},{68,180},{69,181},{70,182},{71... | collective-permute-start | bytes 196616 | tf_op jit(solution)/shard_map/ppermute | solution.py:266
  84.8 2.8 collective-permute-start.8
  85.5 2.1 collective-permute-start.9
  88.9 2.7 collective-permute-start.11
  89.6 2.0 collective-permute-start.12
  92.1 2.7 collective-permute-start.15
  92.8 2.0 collective-permute-start.16
  95.2 2.7 collective-permute-start.19
  95.9 2.0 collective-permute-start.20
  98.3 2.9 collective-permute-start.23
  99.0 2.2 collective-permute-start.24
  99.7 1.5 collective-permute-start.25
  101.6 184.0 %collective-permute-start.27 = (bf16[128,384]{1,0:T(8,128)(2,1)S(1)}, bf16[128,384]{1,0:T(8,128)(2,1)S(1)}, u32[]{:S(2)}, u32[]{:S(2)}) collective-permute-start(bf16[128,384]{1,0:T(8,128)(2,1)S(1)} %get-tuple-element.279), channel_id=1, source_target_pairs={{384,448},{385,449},{386,450},{387,451},{388,452},{389,453},{390,4... | collective-permute-start | bytes 294920 | tf_op jit(solution)/shard_map/ppermute | solution.py:266
  102.9 181.0 %collective-permute-start.28 = (bf16[128,256]{1,0:T(8,128)(2,1)S(1)}, bf16[128,256]{1,0:T(8,128)(2,1)S(1)}, u32[]{:S(2)}, u32[]{:S(2)}) collective-permute-start(bf16[128,256]{1,0:T(8,128)(2,1)S(1)} %get-tuple-element.280), channel_id=1, source_target_pairs={{384,464},{385,465},{386,466},{387,467},{388,468},{389,469},{390,4... | collective-permute-start | bytes 196616 | tf_op jit(solution)/shard_map/ppermute | solution.py:266
  104.2 181.3 %collective-permute-start.29 = (bf16[128,256]{1,0:T(8,128)(2,1)S(1)}, bf16[128,256]{1,0:T(8,128)(2,1)S(1)}, u32[]{:S(2)}, u32[]{:S(2)}) collective-permute-start(bf16[128,256]{1,0:T(8,128)(2,1)S(1)} %get-tuple-element.281), channel_id=1, source_target_pairs={{384,480},{385,481},{386,482},{387,483},{388,484},{389,485},{390,4... | collective-permute-start | bytes 196616 | tf_op jit(solution)/shard_map/ppermute | solution.py:266
  105.5 180.1 %collective-permute-start.30 = (bf16[128,256]{1,0:T(8,128)(2,1)S(1)}, bf16[128,256]{1,0:T(8,128)(2,1)S(1)}, u32[]{:S(2)}, u32[]{:S(2)}) collective-permute-start(bf16[128,256]{1,0:T(8,128)(2,1)S(1)} %get-tuple-element.282), channel_id=1, source_target_pairs={{384,496},{385,497},{386,498},{387,499},{388,500},{389,501},{390,5... | collective-permute-start | bytes 196616 | tf_op jit(solution)/shard_map/ppermute | solution.py:266
  (18 other events, 134.5 us)

commit v4 on v3

--- a/solution.py
+++ b/solution.py
@@ -201,9 +201,13 @@
     )(x, own, gain, weights, keep, inverse)
 
 
-def to_next(section, shift):
+def to_next(section, shift, answer):
+    moves = [(section, section + 1)]
+    if answer and section in (2, 4, 6):
+        moves.append((section - 1, section - 2))
     return [
-        (section * Y * Z + y * Z + z, (section + 1) * Y * Z + ((y + shift) % Y) * Z + z)
+        (source * Y * Z + y * Z + z, target * Y * Z + ((y + shift) % Y) * Z + z)
+        for source, target in moves
         for y in range(Y)
         for z in range(Z)
     ]
@@ -242,7 +246,7 @@
 
     own = stream_in
     mine = lax.cond(
-        section != 1,
+        (section == 0) | (section >= 4),
         gather_z,
         lambda o: jnp.zeros((Z, TOKENS, BLOCK), BF),
         jnp.where(section == 0, own, inverse_own),
@@ -263,19 +267,19 @@
 
         mine, *messages = lax.cond(here, active, idle, mine, own, *kept)
         my_own = jnp.where(here, own, my_own)
-        parts = [lax.ppermute(m, AXES, to_next(phase, k)) for k, m in enumerate(messages)]
+        parts = [lax.ppermute(m, AXES, to_next(phase, k, k == 0)) for k, m in enumerate(messages)]
         if phase == 0:
             messages, inverse_z = lax.optimization_barrier((messages, inverse_z))
-            inverse = lax.cond(section >= 2, lambda z, i: gather_y(z), lambda z, i: i, inverse_z, inverse)
+            inverse = lax.cond(section >= 4, lambda z, i: gather_y(z), lambda z, i: i, inverse_z, inverse)
             parts, inverse = lax.optimization_barrier((parts, inverse))
         if phase == 1:
             messages, mask_rows = lax.optimization_barrier((messages, mask_rows))
             keep = spread_masks(mask_rows)
             parts, keep = lax.optimization_barrier((parts, keep))
-        if phase == 2:
+        if phase in (3, 5):
             messages, inverse_own = lax.optimization_barrier((messages, inverse_own))
             inverse = lax.cond(
-                section < 2, lambda b, i: gather_y(gather_z(b)), lambda b, i: i, inverse_own, inverse
+                (section == phase - 3) | (section == phase - 2), lambda b, i: gather_y(gather_z(b)), lambda b, i: i, inverse_own, inverse
             )
             parts, inverse = lax.optimization_barrier((parts, inverse))
         own = join(parts)

time: 338 us -> 329 us (0.973)
  waiting for transfers between devices: 179 us -> 170 us
    ppermute x28, waiting for transfers between devices: 179 us -> 170 us  [body(): lax.ppermute(m, AXES, to_next(phase, k, k == 0))]
where the time goes in v4:
time: 329 us; the launch traced here: 328 us
  waiting for transfers between devices  170 us (52%)
  blocking collectives  106 us (32%)
  starting transfers between devices  30.8 us (9%)
  Pallas kernels  10.4 us (3%)
  local copies, waits for them, and re-layouts  7.02 us (2%)
    ppermute x28, waiting for transfers between devices, body(): lax.ppermute(m, AXES, to_next(phase, k, k == 0))  170 us
    all_to_all x2, blocking collectives, gather_z(): return lax.all_to_all(copies, 'dp', 0, 0, axis_index_groups=Z_GROUPS)  63.4 us
    all_to_all x2, blocking collectives, gather_y(): got = lax.all_to_all(copies, 'dp', 0, 0, axis_index_groups=Y_GROUPS)  42.5 us
    ppermute x28, starting transfers between devices, body(): lax.ppermute(m, AXES, to_next(phase, k, k == 0))  21.1 us
    ppermute x3, starting transfers between devices, body(): lax.ppermute(kept[Y - k], AXES, along_y(Y - k))  9.62 us
  transfers between devices with their start and end apart: 31, of which 3 were waited for; matrix products, arithmetic and copies ran while one was open for 1% of the time, Pallas kernels for 1%

profile of v4, /device:TPU:39, one launch (start us, length us, event | category | flops | bytes accessed | tf_op | source)
XLA Modules:
  0.0 328.2 jit_solution(17797590224790194320)
XLA Ops:
  0.7 1.6 copy-done
  3.4 4.8 %collective-permute-start = (bf16[128,2048]{1,0:T(8,128)(2,1)S(1)}, bf16[128,2048]{1,0:T(8,128)(2,1)}, u32[]{:S(2)}, u32[]{:S(2)}) collective-permute-start(bf16[128,2048]{1,0:T(8,128)(2,1)S(1)} %keep_weights.5), channel_id=1, source_target_pairs={{0,48},{1,49},{2,50},{3,51},{4,52},{5,53},{6,54},{7,55},{8,56},{9,... | collective-permute-start | bytes 1572872 | tf_op jit(solution)/shard_map/ppermute | solution.py:243
  8.6 2.3 collective-permute-start.1
  10.9 1.1 keep_weights.7
  12.0 2.6 collective-permute-start.2
  14.6 1.1 keep_weights.4
  15.8 39.1 %conditional.12 = (bf16[16,128,128]{2,1,0:T(8,128)(2,1)}) conditional(s32[]{:T(128)} %convert_element_type.346, () %tuple.101, (pred[]{:T(512)}, bf16[128,128]{1,0:T(8,128)(2,1)S(1)}, bf16[128,128]{1,0:T(8,128)(2,1)S(1)}) %tuple.154), branch_computations={%region_0.1_spmd, %region_1.2_spmd} | conditional | flops 16384 | bytes 1703945 | solution.py:248
  15.9 39.0 %all_to_all.57 = bf16[16,128,128]{2,1,0:T(8,128)(2,1)} all-to-all(bf16[16,128,128]{2,1,0:T(8,128)(2,1)S(1)} %broadcast_in_dim.34), channel_id=1, replica_groups={{0,1,2,3,4,5,6,7,8,9,10,11,12,13,14,15},{16,17,18,19,20,21,22,23,24,25,..., dimensions={0} | all-to-all | bytes 1048576 | tf_op jit(solution)/shard_map/cond/branch_1_fun/all_to_all | solution.py:239
  57.7 25.3 %conditional.14 = (bf16[64,128,128]{2,1,0:T(8,128)(2,1)}) conditional(s32[]{:T(128)} %convert_element_type.350, () %tuple.104, bf16[16,128,128]{2,1,0:T(8,128)(2,1)} %get-tuple-element.378), branch_computations={%region_4.5_spmd, %region_5.6_spmd} | conditional | bytes 6815752 | solution.py:273
  57.7 1.6 broadcast_in_dim.36
  59.3 23.7 %all_to_all.58 = bf16[4,16,128,128]{3,2,1,0:T(8,128)(2,1)} all-to-all(bf16[4,16,128,128]{3,2,1,0:T(8,128)(2,1)S(1)} %broadcast_in_dim.36), channel_id=1, replica_groups={{0,16,32,48},{1,17,33,49},{2,18,34,50},{3,19,35,51},{4,20,36,52},{5,21,..., dimensions={0} | all-to-all | bytes 4194304 | tf_op jit(solution)/shard_map/cond/branch_1_fun/all_to_all | solution.py:234
  86.1 1.4 spread_masks.1.keep_ref
  87.9 1.0 copy-done.2
  101.6 1.3 collective-permute-start.27
  102.9 1.3 collective-permute-start.28
  104.2 1.3 collective-permute-start.29
  105.5 1.3 collective-permute-start.30
  106.8 168.4 %collective-permute-done.28 = bf16[128,256]{1,0:T(8,128)(2,1)S(1)} collective-permute-done((bf16[128,256]{1,0:T(8,128)(2,1)S(1)}, bf16[128,256]{1,0:T(8,128)(2,1)S(1)}, u32[]{:S(2)}, u32[]{:S(2)}) %collective-permute-start.28) | collective-permute-done | bytes 65568 | tf_op jit(solution)/shard_map/ppermute | solution.py:270
  275.3 1.6 collective-permute-done.29
  277.2 24.5 %conditional.23 = (bf16[16,128,128]{2,1,0:T(8,128)(2,1)}) conditional(s32[]{:T(128)} %convert_element_type.339, bf16[16,128,128]{2,1,0:T(8,128)(2,1)} %get-tuple-element.295, bf16[128,128]{1,0:T(8,128)(2,1)S(1)} %get-tuple-element.309), branch_computations={%region_22.23_spmd, %region_23.24_spmd} | conditional | bytes 1605640 | solution.py:288
  277.4 24.4 %all_to_all.69 = bf16[16,128,128]{2,1,0:T(8,128)(2,1)} all-to-all(bf16[16,128,128]{2,1,0:T(8,128)(2,1)S(1)} %broadcast_in_dim.59), channel_id=1, replica_groups={{0,1,2,3,4,5,6,7,8,9,10,11,12,13,14,15},{16,17,18,19,20,21,22,23,24,25,..., dimensions={0} | all-to-all | bytes 1048576 | tf_op jit(solution)/shard_map/cond/branch_1_fun/all_to_all | solution.py:239
  301.8 1.5 broadcast_in_dim.67
  303.3 18.8 %all_to_all.70 = bf16[4,16,128,128]{3,2,1,0:T(8,128)(2,1)S(1)} all-to-all(bf16[4,16,128,128]{3,2,1,0:T(8,128)(2,1)S(1)} %broadcast_in_dim.67), channel_id=1, replica_groups={{0,16,32,48},{1,17,33,49},{2,18,34,50},{3,19,35,51},{4,20,36,52},{5,21,..., dimensions={0} | all-to-all | bytes 4194304 | tf_op jit(solution)/shard_map/all_to_all | solution.py:234
  322.1 6.1 %refit.1 = (bf16[128,128]{1,0:T(8,128)(2,1)}, bf16[128,8192]{1,0:T(8,128)(2,1)}) custom-call(bf16[64,128,128]{2,1,0:T(8,128)(2,1)S(1)} %bitcast.19, bf16[128,128]{1,0:T(8,128)(2,1)S(1)} %get-tuple-element.308.own_ref, f32[1,8192]{1,0:T(1,128)S(1)} %copy-done.6, bf16[128,8192]{1,0:T(8,128)(2,1)S(1)} %bitcast.18, bf16[128,8192]{1,0:T(8,128)(2,1)S(1)} %copy-done.3, ...), custom_call_target="tpu_custom_call" | custom-call | tf_op jit(solution)/shard_map/refit/pallas_call | solution.py:181
  (131 shorter events, 20.9 us)
Async XLA Ops:
  3.4 51.5 %collective-permute-start = (bf16[128,2048]{1,0:T(8,128)(2,1)S(1)}, bf16[128,2048]{1,0:T(8,128)(2,1)}, u32[]{:S(2)}, u32[]{:S(2)}) collective-permute-start(bf16[128,2048]{1,0:T(8,128)(2,1)S(1)} %keep_weights.5), channel_id=1, source_target_pairs={{0,48},{1,49},{2,50},{3,51},{4,52},{5,53},{6,54},{7,55},{8,56},{9,... | collective-permute-start | bytes 1572872 | tf_op jit(solution)/shard_map/ppermute | solution.py:243
  8.6 46.4 %collective-permute-start.1 = (bf16[128,2048]{1,0:T(8,128)(2,1)S(1)}, bf16[128,2048]{1,0:T(8,128)(2,1)}, u32[]{:S(2)}, u32[]{:S(2)}) collective-permute-start(bf16[128,2048]{1,0:T(8,128)(2,1)S(1)} %keep_weights.6), channel_id=1, source_target_pairs={{0,32},{1,33},{2,34},{3,35},{4,36},{5,37},{6,38},{7,39},{8,40},{9,... | collective-permute-start | bytes 1572872 | tf_op jit(solution)/shard_map/ppermute | solution.py:243
  12.0 42.9 %collective-permute-start.2 = (bf16[128,2048]{1,0:T(8,128)(2,1)}, bf16[128,2048]{1,0:T(8,128)(2,1)}, u32[]{:S(2)}, u32[]{:S(2)}) collective-permute-start(bf16[128,2048]{1,0:T(8,128)(2,1)} %keep_weights.7), channel_id=1, source_target_pairs={{0,16},{1,17},{2,18},{3,19},{4,20},{5,21},{6,22},{7,23},{8,24},{9,... | collective-permute-start | bytes 1572872 | tf_op jit(solution)/shard_map/ppermute | solution.py:243
  55.0 28.0 %collective-permute-start.3 = (bf16[128,384]{1,0:T(8,128)(2,1)S(1)}, bf16[128,384]{1,0:T(8,128)(2,1)S(1)}, u32[]{:S(2)}, u32[]{:S(2)}) collective-permute-start(bf16[128,384]{1,0:T(8,128)(2,1)S(1)} %get-tuple-element.244), channel_id=1, source_target_pairs={{0,64},{1,65},{2,66},{3,67},{4,68},{5,69},{6,70},{7,71},{8,72},{9,... | collective-permute-start | bytes 294920 | tf_op jit(solution)/shard_map/ppermute | solution.py:270
  55.7 27.3 %collective-permute-start.4 = (bf16[128,256]{1,0:T(8,128)(2,1)S(1)}, bf16[128,256]{1,0:T(8,128)(2,1)S(1)}, u32[]{:S(2)}, u32[]{:S(2)}) collective-permute-start(bf16[128,256]{1,0:T(8,128)(2,1)S(1)} %get-tuple-element.245), channel_id=1, source_target_pairs={{0,80},{1,81},{2,82},{3,83},{4,84},{5,85},{6,86},{7,87},{8,88},{9,... | collective-permute-start | bytes 196616 | tf_op jit(solution)/shard_map/ppermute | solution.py:270
  56.4 26.7 %collective-permute-start.5 = (bf16[128,256]{1,0:T(8,128)(2,1)S(1)}, bf16[128,256]{1,0:T(8,128)(2,1)S(1)}, u32[]{:S(2)}, u32[]{:S(2)}) collective-permute-start(bf16[128,256]{1,0:T(8,128)(2,1)S(1)} %get-tuple-element.246), channel_id=1, source_target_pairs={{0,96},{1,97},{2,98},{3,99},{4,100},{5,101},{6,102},{7,103},{8,104... | collective-permute-start | bytes 196616 | tf_op jit(solution)/shard_map/ppermute | solution.py:270
  57.0 26.0 %collective-permute-start.6 = (bf16[128,256]{1,0:T(8,128)(2,1)S(1)}, bf16[128,256]{1,0:T(8,128)(2,1)S(1)}, u32[]{:S(2)}, u32[]{:S(2)}) collective-permute-start(bf16[128,256]{1,0:T(8,128)(2,1)S(1)} %get-tuple-element.247), channel_id=1, source_target_pairs={{0,112},{1,113},{2,114},{3,115},{4,116},{5,117},{6,118},{7,119},{8... | collective-permute-start | bytes 196616 | tf_op jit(solution)/shard_map/ppermute | solution.py:270
  83.4 4.2 %collective-permute-start.7 = (bf16[128,384]{1,0:T(8,128)(2,1)S(1)}, bf16[128,384]{1,0:T(8,128)(2,1)S(1)}, u32[]{:S(2)}, u32[]{:S(2)}) collective-permute-start(bf16[128,384]{1,0:T(8,128)(2,1)S(1)} %get-tuple-element.254), channel_id=1, source_target_pairs={{64,128},{65,129},{66,130},{67,131},{68,132},{69,133},{70,134},{71... | collective-permute-start | bytes 294920 | tf_op jit(solution)/shard_map/ppermute | solution.py:270
  84.1 3.5 %collective-permute-start.10 = (bf16[128,256]{1,0:T(8,128)(2,1)S(1)}, bf16[128,256]{1,0:T(8,128)(2,1)S(1)}, u32[]{:S(2)}, u32[]{:S(2)}) collective-permute-start(bf16[128,256]{1,0:T(8,128)(2,1)S(1)} %get-tuple-element.257), channel_id=1, source_target_pairs={{64,176},{65,177},{66,178},{67,179},{68,180},{69,181},{70,182},{71... | collective-permute-start | bytes 196616 | tf_op jit(solution)/shard_map/ppermute | solution.py:270
  84.8 2.8 collective-permute-start.8
  85.5 2.1 collective-permute-start.9
  88.9 2.7 collective-permute-start.11
  89.6 2.0 collective-permute-start.12
  92.1 2.8 collective-permute-start.15
  92.7 2.0 collective-permute-start.16
  95.2 2.7 collective-permute-start.19
  95.9 2.0 collective-permute-start.20
  98.3 2.9 collective-permute-start.23
  99.0 2.2 collective-permute-start.24
  99.7 1.6 collective-permute-start.25
  101.6 175.3 %collective-permute-start.27 = (bf16[128,384]{1,0:T(8,128)(2,1)S(1)}, bf16[128,384]{1,0:T(8,128)(2,1)S(1)}, u32[]{:S(2)}, u32[]{:S(2)}) collective-permute-start(bf16[128,384]{1,0:T(8,128)(2,1)S(1)} %get-tuple-element.296), channel_id=1, source_target_pairs={{384,448},{385,449},{386,450},{387,451},{388,452},{389,453},{390,4... | collective-permute-start | bytes 294920 | tf_op jit(solution)/shard_map/ppermute | solution.py:270
  102.9 172.3 %collective-permute-start.28 = (bf16[128,256]{1,0:T(8,128)(2,1)S(1)}, bf16[128,256]{1,0:T(8,128)(2,1)S(1)}, u32[]{:S(2)}, u32[]{:S(2)}) collective-permute-start(bf16[128,256]{1,0:T(8,128)(2,1)S(1)} %get-tuple-element.297), channel_id=1, source_target_pairs={{384,464},{385,465},{386,466},{387,467},{388,468},{389,469},{390,4... | collective-permute-start | bytes 196616 | tf_op jit(solution)/shard_map/ppermute | solution.py:270
  104.2 172.6 %collective-permute-start.29 = (bf16[128,256]{1,0:T(8,128)(2,1)S(1)}, bf16[128,256]{1,0:T(8,128)(2,1)S(1)}, u32[]{:S(2)}, u32[]{:S(2)}) collective-permute-start(bf16[128,256]{1,0:T(8,128)(2,1)S(1)} %get-tuple-element.298), channel_id=1, source_target_pairs={{384,480},{385,481},{386,482},{387,483},{388,484},{389,485},{390,4... | collective-permute-start | bytes 196616 | tf_op jit(solution)/shard_map/ppermute | solution.py:270
  105.5 171.4 %collective-permute-start.30 = (bf16[128,256]{1,0:T(8,128)(2,1)S(1)}, bf16[128,256]{1,0:T(8,128)(2,1)S(1)}, u32[]{:S(2)}, u32[]{:S(2)}) collective-permute-start(bf16[128,256]{1,0:T(8,128)(2,1)S(1)} %get-tuple-element.299), channel_id=1, source_target_pairs={{384,496},{385,497},{386,498},{387,499},{388,500},{389,501},{390,5... | collective-permute-start | bytes 196616 | tf_op jit(solution)/shard_map/ppermute | solution.py:270
  (18 other events, 134.5 us)

commit v5 on v4

--- a/solution.py
+++ b/solution.py
@@ -61,7 +61,8 @@
 
 
 def layer_kernel(x_ref, own_ref, gain_ref, *refs):
-    kept_refs, outs, scaled = refs[:Y], refs[Y : 2 * Y], refs[2 * Y]
+    kept_refs, outs, scaled = refs[: -Y - 1], refs[-Y - 1 : -1], refs[-1]
+    pieces = kept_refs if len(kept_refs) == Y else [kept_refs[0].at[k] for k in range(Y)]
     squares = jnp.zeros((TOKENS, BLOCK), F32)
     for j in range(Z):
         x = x_ref[j].astype(F32)
@@ -80,7 +81,7 @@
     ).astype(BF)
     for k in range(Y):
         partial = lax.dot_general(
-            scaled[...], kept_refs[k][...], NT, preferred_element_type=F32
+            scaled[...], pieces[k][...], NT, preferred_element_type=F32
         )
         outs[k][:, :BLOCK] = (partial * SCALE).astype(BF)
         outs[k][:, BLOCK : 2 * BLOCK] = both
@@ -269,9 +270,10 @@
         my_own = jnp.where(here, own, my_own)
         parts = [lax.ppermute(m, AXES, to_next(phase, k, k == 0)) for k, m in enumerate(messages)]
         if phase == 0:
-            messages, inverse_z = lax.optimization_barrier((messages, inverse_z))
+            messages, inverse_z, kept = lax.optimization_barrier((messages, inverse_z, kept))
+            kept = [jnp.stack(kept)]
             inverse = lax.cond(section >= 4, lambda z, i: gather_y(z), lambda z, i: i, inverse_z, inverse)
-            parts, inverse = lax.optimization_barrier((parts, inverse))
+            parts, inverse, kept = lax.optimization_barrier((parts, inverse, kept))
         if phase == 1:
             messages, mask_rows = lax.optimization_barrier((messages, mask_rows))
             keep = spread_masks(mask_rows)

time: 329 us -> 330 us (level)
  no operation moved by 1% of the time
where the time goes in v5:
time: 330 us; the launch traced here: 329 us
  waiting for transfers between devices  168 us (51%)
  blocking collectives  106 us (32%)
  starting transfers between devices  30.9 us (9%)
  Pallas kernels  10.4 us (3%)
  local copies, waits for them, and re-layouts  6.99 us (2%)
  other arithmetic  5.12 us (2%)
    ppermute x28, waiting for transfers between devices, body(): lax.ppermute(m, AXES, to_next(phase, k, k == 0))  168 us
    all_to_all x2, blocking collectives, gather_z(): return lax.all_to_all(copies, 'dp', 0, 0, axis_index_groups=Z_GROUPS)  63.4 us
    all_to_all x2, blocking collectives, gather_y(): got = lax.all_to_all(copies, 'dp', 0, 0, axis_index_groups=Y_GROUPS)  42.5 us
    ppermute x28, starting transfers between devices, body(): lax.ppermute(m, AXES, to_next(phase, k, k == 0))  21.3 us
    ppermute x3, starting transfers between devices, body(): lax.ppermute(kept[Y - k], AXES, along_y(Y - k))  9.62 us
  transfers between devices with their start and end apart: 31, of which 3 were waited for; matrix products, arithmetic and copies ran while one was open for 1% of the time, Pallas kernels for 1%

profile of v5, /device:TPU:39, one launch (start us, length us, event | category | flops | bytes accessed | tf_op | source)
XLA Modules:
  0.0 329.2 jit_solution(9372626624950582591)
XLA Ops:
  0.7 1.6 copy-done
  3.4 4.8 %collective-permute-start = (bf16[128,2048]{1,0:T(8,128)(2,1)S(1)}, bf16[128,2048]{1,0:T(8,128)(2,1)}, u32[]{:S(2)}, u32[]{:S(2)}) collective-permute-start(bf16[128,2048]{1,0:T(8,128)(2,1)S(1)} %keep_weights.5), channel_id=1, source_target_pairs={{0,48},{1,49},{2,50},{3,51},{4,52},{5,53},{6,54},{7,55},{8,56},{9,... | collective-permute-start | bytes 1572872 | tf_op jit(solution)/shard_map/ppermute | solution.py:244
  8.6 2.3 collective-permute-start.1
  10.9 1.1 keep_weights.7
  12.0 2.6 collective-permute-start.2
  14.6 1.1 keep_weights.4
  15.8 39.1 %conditional.12 = (bf16[16,128,128]{2,1,0:T(8,128)(2,1)}) conditional(s32[]{:T(128)} %convert_element_type.346, () %tuple.101, (pred[]{:T(512)}, bf16[128,128]{1,0:T(8,128)(2,1)S(1)}, bf16[128,128]{1,0:T(8,128)(2,1)S(1)}) %tuple.149), branch_computations={%region_0.1_spmd, %region_1.2_spmd} | conditional | flops 16384 | bytes 1703945 | solution.py:249
  15.9 39.0 %all_to_all.57 = bf16[16,128,128]{2,1,0:T(8,128)(2,1)} all-to-all(bf16[16,128,128]{2,1,0:T(8,128)(2,1)S(1)} %broadcast_in_dim.34), channel_id=1, replica_groups={{0,1,2,3,4,5,6,7,8,9,10,11,12,13,14,15},{16,17,18,19,20,21,22,23,24,25,..., dimensions={0} | all-to-all | bytes 1048576 | tf_op jit(solution)/shard_map/cond/branch_1_fun/all_to_all | solution.py:240
  57.7 3.1 pad_maximum_fusion
  60.8 25.2 %conditional.14 = (bf16[64,128,128]{2,1,0:T(8,128)(2,1)}) conditional(s32[]{:T(128)} %convert_element_type.350, () %tuple.104, bf16[16,128,128]{2,1,0:T(8,128)(2,1)} %get-tuple-element.334), branch_computations={%region_4.5_spmd, %region_5.6_spmd} | conditional | bytes 6815752 | solution.py:275
  60.8 1.5 broadcast_in_dim.36
  62.4 23.7 %all_to_all.58 = bf16[4,16,128,128]{3,2,1,0:T(8,128)(2,1)} all-to-all(bf16[4,16,128,128]{3,2,1,0:T(8,128)(2,1)S(1)} %broadcast_in_dim.36), channel_id=1, replica_groups={{0,16,32,48},{1,17,33,49},{2,18,34,50},{3,19,35,51},{4,20,36,52},{5,21,..., dimensions={0} | all-to-all | bytes 4194304 | tf_op jit(solution)/shard_map/cond/branch_1_fun/all_to_all | solution.py:235
  89.2 1.4 spread_masks.1.keep_ref
  104.7 1.3 collective-permute-start.27
  106.0 1.3 collective-permute-start.28
  107.3 1.3 collective-permute-start.29
  108.6 1.3 collective-permute-start.30
  109.9 166.3 %collective-permute-done.28 = bf16[128,256]{1,0:T(8,128)(2,1)S(1)} collective-permute-done((bf16[128,256]{1,0:T(8,128)(2,1)S(1)}, bf16[128,256]{1,0:T(8,128)(2,1)S(1)}, u32[]{:S(2)}, u32[]{:S(2)}) %collective-permute-start.28) | collective-permute-done | bytes 65568 | tf_op jit(solution)/shard_map/ppermute | solution.py:271
  276.2 1.6 collective-permute-done.29
  278.2 24.5 %conditional.23 = (bf16[16,128,128]{2,1,0:T(8,128)(2,1)}) conditional(s32[]{:T(128)} %convert_element_type.339, bf16[16,128,128]{2,1,0:T(8,128)(2,1)} %get-tuple-element.251, bf16[128,128]{1,0:T(8,128)(2,1)S(1)} %get-tuple-element.265), branch_computations={%region_22.23_spmd, %region_23.24_spmd} | conditional | bytes 1605640 | solution.py:290
  278.3 24.4 %all_to_all.69 = bf16[16,128,128]{2,1,0:T(8,128)(2,1)} all-to-all(bf16[16,128,128]{2,1,0:T(8,128)(2,1)S(1)} %broadcast_in_dim.59), channel_id=1, replica_groups={{0,1,2,3,4,5,6,7,8,9,10,11,12,13,14,15},{16,17,18,19,20,21,22,23,24,25,..., dimensions={0} | all-to-all | bytes 1048576 | tf_op jit(solution)/shard_map/cond/branch_1_fun/all_to_all | solution.py:240
  302.7 1.5 broadcast_in_dim.67
  304.3 18.8 %all_to_all.70 = bf16[4,16,128,128]{3,2,1,0:T(8,128)(2,1)S(1)} all-to-all(bf16[4,16,128,128]{3,2,1,0:T(8,128)(2,1)S(1)} %broadcast_in_dim.67), channel_id=1, replica_groups={{0,16,32,48},{1,17,33,49},{2,18,34,50},{3,19,35,51},{4,20,36,52},{5,21,..., dimensions={0} | all-to-all | bytes 4194304 | tf_op jit(solution)/shard_map/all_to_all | solution.py:235
  323.1 6.1 %refit.1 = (bf16[128,128]{1,0:T(8,128)(2,1)}, bf16[128,8192]{1,0:T(8,128)(2,1)}) custom-call(bf16[64,128,128]{2,1,0:T(8,128)(2,1)S(1)} %bitcast.23, bf16[128,128]{1,0:T(8,128)(2,1)S(1)} %get-tuple-element.264.own_ref, f32[1,8192]{1,0:T(1,128)S(1)} %copy-done.6, bf16[128,8192]{1,0:T(8,128)(2,1)S(1)} %bitcast.22, bf16[128,8192]{1,0:T(8,128)(2,1)S(1)} %copy-done.3, ...), custom_call_target="tpu_custom_call" | custom-call | tf_op jit(solution)/shard_map/refit/pallas_call | solution.py:182
  (132 shorter events, 21.9 us)
Async XLA Ops:
  3.4 51.5 %collective-permute-start = (bf16[128,2048]{1,0:T(8,128)(2,1)S(1)}, bf16[128,2048]{1,0:T(8,128)(2,1)}, u32[]{:S(2)}, u32[]{:S(2)}) collective-permute-start(bf16[128,2048]{1,0:T(8,128)(2,1)S(1)} %keep_weights.5), channel_id=1, source_target_pairs={{0,48},{1,49},{2,50},{3,51},{4,52},{5,53},{6,54},{7,55},{8,56},{9,... | collective-permute-start | bytes 1572872 | tf_op jit(solution)/shard_map/ppermute | solution.py:244
  8.6 46.4 %collective-permute-start.1 = (bf16[128,2048]{1,0:T(8,128)(2,1)S(1)}, bf16[128,2048]{1,0:T(8,128)(2,1)}, u32[]{:S(2)}, u32[]{:S(2)}) collective-permute-start(bf16[128,2048]{1,0:T(8,128)(2,1)S(1)} %keep_weights.6), channel_id=1, source_target_pairs={{0,32},{1,33},{2,34},{3,35},{4,36},{5,37},{6,38},{7,39},{8,40},{9,... | collective-permute-start | bytes 1572872 | tf_op jit(solution)/shard_map/ppermute | solution.py:244
  12.0 43.0 %collective-permute-start.2 = (bf16[128,2048]{1,0:T(8,128)(2,1)}, bf16[128,2048]{1,0:T(8,128)(2,1)}, u32[]{:S(2)}, u32[]{:S(2)}) collective-permute-start(bf16[128,2048]{1,0:T(8,128)(2,1)} %keep_weights.7), channel_id=1, source_target_pairs={{0,16},{1,17},{2,18},{3,19},{4,20},{5,21},{6,22},{7,23},{8,24},{9,... | collective-permute-start | bytes 1572872 | tf_op jit(solution)/shard_map/ppermute | solution.py:244
  55.0 31.0 %collective-permute-start.3 = (bf16[128,384]{1,0:T(8,128)(2,1)S(1)}, bf16[128,384]{1,0:T(8,128)(2,1)S(1)}, u32[]{:S(2)}, u32[]{:S(2)}) collective-permute-start(bf16[128,384]{1,0:T(8,128)(2,1)S(1)} %get-tuple-element.195), channel_id=1, source_target_pairs={{0,64},{1,65},{2,66},{3,67},{4,68},{5,69},{6,70},{7,71},{8,72},{9,... | collective-permute-start | bytes 294920 | tf_op jit(solution)/shard_map/ppermute | solution.py:271
  55.7 30.3 %collective-permute-start.4 = (bf16[128,256]{1,0:T(8,128)(2,1)S(1)}, bf16[128,256]{1,0:T(8,128)(2,1)S(1)}, u32[]{:S(2)}, u32[]{:S(2)}) collective-permute-start(bf16[128,256]{1,0:T(8,128)(2,1)S(1)} %get-tuple-element.196), channel_id=1, source_target_pairs={{0,80},{1,81},{2,82},{3,83},{4,84},{5,85},{6,86},{7,87},{8,88},{9,... | collective-permute-start | bytes 196616 | tf_op jit(solution)/shard_map/ppermute | solution.py:271
  56.4 29.7 %collective-permute-start.5 = (bf16[128,256]{1,0:T(8,128)(2,1)S(1)}, bf16[128,256]{1,0:T(8,128)(2,1)S(1)}, u32[]{:S(2)}, u32[]{:S(2)}) collective-permute-start(bf16[128,256]{1,0:T(8,128)(2,1)S(1)} %get-tuple-element.197), channel_id=1, source_target_pairs={{0,96},{1,97},{2,98},{3,99},{4,100},{5,101},{6,102},{7,103},{8,104... | collective-permute-start | bytes 196616 | tf_op jit(solution)/shard_map/ppermute | solution.py:271
  57.0 29.0 %collective-permute-start.6 = (bf16[128,256]{1,0:T(8,128)(2,1)S(1)}, bf16[128,256]{1,0:T(8,128)(2,1)S(1)}, u32[]{:S(2)}, u32[]{:S(2)}) collective-permute-start(bf16[128,256]{1,0:T(8,128)(2,1)S(1)} %get-tuple-element.198), channel_id=1, source_target_pairs={{0,112},{1,113},{2,114},{3,115},{4,116},{5,117},{6,118},{7,119},{8... | collective-permute-start | bytes 196616 | tf_op jit(solution)/shard_map/ppermute | solution.py:271
  86.5 4.2 %collective-permute-start.7 = (bf16[128,384]{1,0:T(8,128)(2,1)S(1)}, bf16[128,384]{1,0:T(8,128)(2,1)S(1)}, u32[]{:S(2)}, u32[]{:S(2)}) collective-permute-start(bf16[128,384]{1,0:T(8,128)(2,1)S(1)} %get-tuple-element.210), channel_id=1, source_target_pairs={{64,128},{65,129},{66,130},{67,131},{68,132},{69,133},{70,134},{71... | collective-permute-start | bytes 294920 | tf_op jit(solution)/shard_map/ppermute | solution.py:271
  87.1 3.5 %collective-permute-start.10 = (bf16[128,256]{1,0:T(8,128)(2,1)S(1)}, bf16[128,256]{1,0:T(8,128)(2,1)S(1)}, u32[]{:S(2)}, u32[]{:S(2)}) collective-permute-start(bf16[128,256]{1,0:T(8,128)(2,1)S(1)} %get-tuple-element.213), channel_id=1, source_target_pairs={{64,176},{65,177},{66,178},{67,179},{68,180},{69,181},{70,182},{71... | collective-permute-start | bytes 196616 | tf_op jit(solution)/shard_map/ppermute | solution.py:271
  87.8 2.8 collective-permute-start.8
  88.5 2.1 collective-permute-start.9
  92.0 2.7 collective-permute-start.11
  92.7 2.0 collective-permute-start.12
  95.1 2.8 collective-permute-start.15
  95.8 2.0 collective-permute-start.16
  96.5 1.4 collective-permute-start.17
  98.3 2.7 collective-permute-start.19
  98.9 2.0 collective-permute-start.20
  101.4 2.9 collective-permute-start.23
  102.2 2.0 collective-permute-start.24
  104.7 173.2 %collective-permute-start.27 = (bf16[128,384]{1,0:T(8,128)(2,1)S(1)}, bf16[128,384]{1,0:T(8,128)(2,1)S(1)}, u32[]{:S(2)}, u32[]{:S(2)}) collective-permute-start(bf16[128,384]{1,0:T(8,128)(2,1)S(1)} %get-tuple-element.252), channel_id=1, source_target_pairs={{384,448},{385,449},{386,450},{387,451},{388,452},{389,453},{390,4... | collective-permute-start | bytes 294920 | tf_op jit(solution)/shard_map/ppermute | solution.py:271
  106.0 170.2 %collective-permute-start.28 = (bf16[128,256]{1,0:T(8,128)(2,1)S(1)}, bf16[128,256]{1,0:T(8,128)(2,1)S(1)}, u32[]{:S(2)}, u32[]{:S(2)}) collective-permute-start(bf16[128,256]{1,0:T(8,128)(2,1)S(1)} %get-tuple-element.253), channel_id=1, source_target_pairs={{384,464},{385,465},{386,466},{387,467},{388,468},{389,469},{390,4... | collective-permute-start | bytes 196616 | tf_op jit(solution)/shard_map/ppermute | solution.py:271
  107.3 170.5 %collective-permute-start.29 = (bf16[128,256]{1,0:T(8,128)(2,1)S(1)}, bf16[128,256]{1,0:T(8,128)(2,1)S(1)}, u32[]{:S(2)}, u32[]{:S(2)}) collective-permute-start(bf16[128,256]{1,0:T(8,128)(2,1)S(1)} %get-tuple-element.254), channel_id=1, source_target_pairs={{384,480},{385,481},{386,482},{387,483},{388,484},{389,485},{390,4... | collective-permute-start | bytes 196616 | tf_op jit(solution)/shard_map/ppermute | solution.py:271
  108.6 169.3 %collective-permute-start.30 = (bf16[128,256]{1,0:T(8,128)(2,1)S(1)}, bf16[128,256]{1,0:T(8,128)(2,1)S(1)}, u32[]{:S(2)}, u32[]{:S(2)}) collective-permute-start(bf16[128,256]{1,0:T(8,128)(2,1)S(1)} %get-tuple-element.255), channel_id=1, source_target_pairs={{384,496},{385,497},{386,498},{387,499},{388,500},{389,501},{390,5... | collective-permute-start | bytes 196616 | tf_op jit(solution)/shard_map/ppermute | solution.py:271
  (18 other events, 110.6 us)

commit v6 on v4

--- a/solution.py
+++ b/solution.py
@@ -17,6 +17,7 @@
 SECTIONS = 8
 SPAN = Z * BLOCK
 SCALE = D ** (-0.5)
+SHIFTS = (2, 1, 3, 0)
 EPS = 1e-05
 AXES = ("section", "dp")
 Y_GROUPS = [[y * Z + z for y in range(Y)] for z in range(Z)]
@@ -78,17 +79,17 @@
         jnp.broadcast_to(high.astype(F32), (TOKENS, BLOCK)),
         jnp.broadcast_to(low.astype(F32), (TOKENS, BLOCK)),
     ).astype(BF)
-    for k in range(Y):
+    for out, k in zip(outs, SHIFTS):
         partial = lax.dot_general(
             scaled[...], kept_refs[k][...], NT, preferred_element_type=F32
         )
-        outs[k][:, :BLOCK] = (partial * SCALE).astype(BF)
-        outs[k][:, BLOCK : 2 * BLOCK] = both
-    outs[0][:, 2 * BLOCK :] = own_ref[...]
+        out[:, :BLOCK] = (partial * SCALE).astype(BF)
+        out[:, BLOCK : 2 * BLOCK] = both
+    outs[-1][:, 2 * BLOCK :] = own_ref[...]
 
 
 def layer(x, own, gain, kept):
-    widths = [3 * BLOCK] + [2 * BLOCK] * (Y - 1)
+    widths = [2 * BLOCK] * (Y - 1) + [3 * BLOCK]
     return pl.pallas_call(
         layer_kernel,
         out_shape=[jax.ShapeDtypeStruct((TOKENS, w), BF) for w in widths],
@@ -105,7 +106,7 @@
         for p in parts
     )
     inverse = lax.rsqrt(total * (1.0 / D) + EPS)
-    return (parts[0][:, 2 * BLOCK :].astype(F32) + projected * inverse).astype(BF)
+    return (parts[-1][:, 2 * BLOCK :].astype(F32) + projected * inverse).astype(BF)
 
 
 def mask_kernel(masks_ref, keep_ref):
@@ -254,7 +255,7 @@
     inverse_z = mine
     my_own = own
     inverse = jnp.zeros((Y * Z, BLOCK, BLOCK), BF)
-    widths = [3 * BLOCK] + [2 * BLOCK] * (Y - 1)
+    widths = [2 * BLOCK] * (Y - 1) + [3 * BLOCK]
     for phase in range(SECTIONS - 1):
         here = section == phase
 
@@ -267,7 +268,9 @@
 
         mine, *messages = lax.cond(here, active, idle, mine, own, *kept)
         my_own = jnp.where(here, own, my_own)
-        parts = [lax.ppermute(m, AXES, to_next(phase, k, k == 0)) for k, m in enumerate(messages)]
+        parts = [
+            lax.ppermute(m, AXES, to_next(phase, k, k == 0)) for m, k in zip(messages, SHIFTS)
+        ]
         if phase == 0:
             messages, inverse_z = lax.optimization_barrier((messages, inverse_z))
             inverse = lax.cond(section >= 4, lambda z, i: gather_y(z), lambda z, i: i, inverse_z, inverse)

time: 329 us -> 328 us (level)
  transfers between devices with their start and end apart: 31 -> 31, of which waited for: 3 -> 2; matrix products, arithmetic and copies ran while one was open for 1% -> 1% of each run, Pallas kernels for 1% -> 1%
where the time goes in v6:
time: 328 us
  waiting for transfers between devices  169 us (52%)
  blocking collectives  106 us (32%)
  starting transfers between devices  30.8 us (9%)
  Pallas kernels  10.4 us (3%)
  local copies, waits for them, and re-layouts  7.02 us (2%)
    ppermute x28, waiting for transfers between devices, body(): lax.ppermute(m, AXES, to_next(phase, k, k == 0))  169 us
    all_to_all x2, blocking collectives, gather_z(): return lax.all_to_all(copies, 'dp', 0, 0, axis_index_groups=Z_GROUPS)  63.4 us
    all_to_all x2, blocking collectives, gather_y(): got = lax.all_to_all(copies, 'dp', 0, 0, axis_index_groups=Y_GROUPS)  42.9 us
    ppermute x28, starting transfers between devices, body(): lax.ppermute(m, AXES, to_next(phase, k, k == 0))  21.1 us
    ppermute x3, starting transfers between devices, body(): lax.ppermute(kept[Y - k], AXES, along_y(Y - k))  9.62 us
  transfers between devices with their start and end apart: 31, of which 2 were waited for; matrix products, arithmetic and copies ran while one was open for 1% of the time, Pallas kernels for 1%

profile of v6, /device:TPU:39, one launch (start us, length us, event | category | flops | bytes accessed | tf_op | source)
XLA Modules:
  0.0 327.5 jit_solution(10510704475255914608)
XLA Ops:
  0.7 1.6 copy-done
  3.4 4.8 %collective-permute-start = (bf16[128,2048]{1,0:T(8,128)(2,1)S(1)}, bf16[128,2048]{1,0:T(8,128)(2,1)}, u32[]{:S(2)}, u32[]{:S(2)}) collective-permute-start(bf16[128,2048]{1,0:T(8,128)(2,1)S(1)} %keep_weights.5), channel_id=1, source_target_pairs={{0,48},{1,49},{2,50},{3,51},{4,52},{5,53},{6,54},{7,55},{8,56},{9,... | collective-permute-start | bytes 1572872 | tf_op jit(solution)/shard_map/ppermute | solution.py:244
  8.6 2.3 collective-permute-start.1
  10.9 1.1 keep_weights.7
  12.0 2.6 collective-permute-start.2
  14.6 1.1 keep_weights.4
  15.8 39.1 %conditional.12 = (bf16[16,128,128]{2,1,0:T(8,128)(2,1)}) conditional(s32[]{:T(128)} %convert_element_type.346, () %tuple.101, (pred[]{:T(512)}, bf16[128,128]{1,0:T(8,128)(2,1)S(1)}, bf16[128,128]{1,0:T(8,128)(2,1)S(1)}) %tuple.154), branch_computations={%region_0.1_spmd, %region_1.2_spmd} | conditional | flops 16384 | bytes 1703945 | solution.py:249
  15.9 39.0 %all_to_all.57 = bf16[16,128,128]{2,1,0:T(8,128)(2,1)} all-to-all(bf16[16,128,128]{2,1,0:T(8,128)(2,1)S(1)} %broadcast_in_dim.34), channel_id=1, replica_groups={{0,1,2,3,4,5,6,7,8,9,10,11,12,13,14,15},{16,17,18,19,20,21,22,23,24,25,..., dimensions={0} | all-to-all | bytes 1048576 | tf_op jit(solution)/shard_map/cond/branch_1_fun/all_to_all | solution.py:240
  57.7 25.3 %conditional.14 = (bf16[64,128,128]{2,1,0:T(8,128)(2,1)}) conditional(s32[]{:T(128)} %convert_element_type.350, () %tuple.104, bf16[16,128,128]{2,1,0:T(8,128)(2,1)} %get-tuple-element.378), branch_computations={%region_4.5_spmd, %region_5.6_spmd} | conditional | bytes 6815752 | solution.py:276
  57.7 1.6 broadcast_in_dim.36
  59.3 23.7 %all_to_all.58 = bf16[4,16,128,128]{3,2,1,0:T(8,128)(2,1)} all-to-all(bf16[4,16,128,128]{3,2,1,0:T(8,128)(2,1)S(1)} %broadcast_in_dim.36), channel_id=1, replica_groups={{0,16,32,48},{1,17,33,49},{2,18,34,50},{3,19,35,51},{4,20,36,52},{5,21,..., dimensions={0} | all-to-all | bytes 4194304 | tf_op jit(solution)/shard_map/cond/branch_1_fun/all_to_all | solution.py:235
  86.1 1.4 spread_masks.1.keep_ref
  87.9 1.0 copy-done.2
  101.6 1.3 collective-permute-start.27
  102.9 1.3 collective-permute-start.28
  104.2 1.3 collective-permute-start.29
  105.5 1.3 collective-permute-start.30
  106.8 167.3 %collective-permute-done.28 = bf16[128,256]{1,0:T(8,128)(2,1)S(1)} collective-permute-done((bf16[128,256]{1,0:T(8,128)(2,1)S(1)}, bf16[128,256]{1,0:T(8,128)(2,1)S(1)}, u32[]{:S(2)}, u32[]{:S(2)}) %collective-permute-start.28) | collective-permute-done | bytes 65568 | tf_op jit(solution)/shard_map/ppermute | solution.py:272
  274.1 1.7 collective-permute-done.29
  276.2 24.5 %conditional.23 = (bf16[16,128,128]{2,1,0:T(8,128)(2,1)}) conditional(s32[]{:T(128)} %convert_element_type.339, bf16[16,128,128]{2,1,0:T(8,128)(2,1)} %get-tuple-element.295, bf16[128,128]{1,0:T(8,128)(2,1)S(1)} %get-tuple-element.309), branch_computations={%region_22.23_spmd, %region_23.24_spmd} | conditional | bytes 1605640 | solution.py:291
  276.3 24.4 %all_to_all.69 = bf16[16,128,128]{2,1,0:T(8,128)(2,1)} all-to-all(bf16[16,128,128]{2,1,0:T(8,128)(2,1)S(1)} %broadcast_in_dim.59), channel_id=1, replica_groups={{0,1,2,3,4,5,6,7,8,9,10,11,12,13,14,15},{16,17,18,19,20,21,22,23,24,25,..., dimensions={0} | all-to-all | bytes 1048576 | tf_op jit(solution)/shard_map/cond/branch_1_fun/all_to_all | solution.py:240
  300.7 1.5 broadcast_in_dim.67
  302.2 19.2 %all_to_all.70 = bf16[4,16,128,128]{3,2,1,0:T(8,128)(2,1)S(1)} all-to-all(bf16[4,16,128,128]{3,2,1,0:T(8,128)(2,1)S(1)} %broadcast_in_dim.67), channel_id=1, replica_groups={{0,16,32,48},{1,17,33,49},{2,18,34,50},{3,19,35,51},{4,20,36,52},{5,21,..., dimensions={0} | all-to-all | bytes 4194304 | tf_op jit(solution)/shard_map/all_to_all | solution.py:235
  321.4 6.1 %refit.1 = (bf16[128,128]{1,0:T(8,128)(2,1)}, bf16[128,8192]{1,0:T(8,128)(2,1)}) custom-call(bf16[64,128,128]{2,1,0:T(8,128)(2,1)S(1)} %bitcast.19, bf16[128,128]{1,0:T(8,128)(2,1)S(1)} %get-tuple-element.308.own_ref, f32[1,8192]{1,0:T(1,128)S(1)} %copy-done.6, bf16[128,8192]{1,0:T(8,128)(2,1)S(1)} %bitcast.18, bf16[128,8192]{1,0:T(8,128)(2,1)S(1)} %copy-done.3, ...), custom_call_target="tpu_custom_call" | custom-call | tf_op jit(solution)/shard_map/refit/pallas_call | solution.py:182
  (131 shorter events, 20.8 us)
Async XLA Ops:
  3.4 51.5 %collective-permute-start = (bf16[128,2048]{1,0:T(8,128)(2,1)S(1)}, bf16[128,2048]{1,0:T(8,128)(2,1)}, u32[]{:S(2)}, u32[]{:S(2)}) collective-permute-start(bf16[128,2048]{1,0:T(8,128)(2,1)S(1)} %keep_weights.5), channel_id=1, source_target_pairs={{0,48},{1,49},{2,50},{3,51},{4,52},{5,53},{6,54},{7,55},{8,56},{9,... | collective-permute-start | bytes 1572872 | tf_op jit(solution)/shard_map/ppermute | solution.py:244
  8.6 46.4 %collective-permute-start.1 = (bf16[128,2048]{1,0:T(8,128)(2,1)S(1)}, bf16[128,2048]{1,0:T(8,128)(2,1)}, u32[]{:S(2)}, u32[]{:S(2)}) collective-permute-start(bf16[128,2048]{1,0:T(8,128)(2,1)S(1)} %keep_weights.6), channel_id=1, source_target_pairs={{0,32},{1,33},{2,34},{3,35},{4,36},{5,37},{6,38},{7,39},{8,40},{9,... | collective-permute-start | bytes 1572872 | tf_op jit(solution)/shard_map/ppermute | solution.py:244
  12.0 42.9 %collective-permute-start.2 = (bf16[128,2048]{1,0:T(8,128)(2,1)}, bf16[128,2048]{1,0:T(8,128)(2,1)}, u32[]{:S(2)}, u32[]{:S(2)}) collective-permute-start(bf16[128,2048]{1,0:T(8,128)(2,1)} %keep_weights.7), channel_id=1, source_target_pairs={{0,16},{1,17},{2,18},{3,19},{4,20},{5,21},{6,22},{7,23},{8,24},{9,... | collective-permute-start | bytes 1572872 | tf_op jit(solution)/shard_map/ppermute | solution.py:244
  55.0 28.0 %collective-permute-start.6 = (bf16[128,384]{1,0:T(8,128)(2,1)S(1)}, bf16[128,384]{1,0:T(8,128)(2,1)S(1)}, u32[]{:S(2)}, u32[]{:S(2)}) collective-permute-start(bf16[128,384]{1,0:T(8,128)(2,1)S(1)} %get-tuple-element.247), channel_id=1, source_target_pairs={{0,64},{1,65},{2,66},{3,67},{4,68},{5,69},{6,70},{7,71},{8,72},{9,... | collective-permute-start | bytes 294920 | tf_op jit(solution)/shard_map/ppermute | solution.py:272
  55.7 27.3 %collective-permute-start.3 = (bf16[128,256]{1,0:T(8,128)(2,1)S(1)}, bf16[128,256]{1,0:T(8,128)(2,1)S(1)}, u32[]{:S(2)}, u32[]{:S(2)}) collective-permute-start(bf16[128,256]{1,0:T(8,128)(2,1)S(1)} %get-tuple-element.244), channel_id=1, source_target_pairs={{0,96},{1,97},{2,98},{3,99},{4,100},{5,101},{6,102},{7,103},{8,104... | collective-permute-start | bytes 196616 | tf_op jit(solution)/shard_map/ppermute | solution.py:272
  56.4 26.7 %collective-permute-start.4 = (bf16[128,256]{1,0:T(8,128)(2,1)S(1)}, bf16[128,256]{1,0:T(8,128)(2,1)S(1)}, u32[]{:S(2)}, u32[]{:S(2)}) collective-permute-start(bf16[128,256]{1,0:T(8,128)(2,1)S(1)} %get-tuple-element.245), channel_id=1, source_target_pairs={{0,80},{1,81},{2,82},{3,83},{4,84},{5,85},{6,86},{7,87},{8,88},{9,... | collective-permute-start | bytes 196616 | tf_op jit(solution)/shard_map/ppermute | solution.py:272
  57.0 26.0 %collective-permute-start.5 = (bf16[128,256]{1,0:T(8,128)(2,1)S(1)}, bf16[128,256]{1,0:T(8,128)(2,1)S(1)}, u32[]{:S(2)}, u32[]{:S(2)}) collective-permute-start(bf16[128,256]{1,0:T(8,128)(2,1)S(1)} %get-tuple-element.246), channel_id=1, source_target_pairs={{0,112},{1,113},{2,114},{3,115},{4,116},{5,117},{6,118},{7,119},{8... | collective-permute-start | bytes 196616 | tf_op jit(solution)/shard_map/ppermute | solution.py:272
  83.4 4.2 %collective-permute-start.10 = (bf16[128,384]{1,0:T(8,128)(2,1)S(1)}, bf16[128,384]{1,0:T(8,128)(2,1)S(1)}, u32[]{:S(2)}, u32[]{:S(2)}) collective-permute-start(bf16[128,384]{1,0:T(8,128)(2,1)S(1)} %get-tuple-element.257), channel_id=1, source_target_pairs={{64,128},{65,129},{66,130},{67,131},{68,132},{69,133},{70,134},{71... | collective-permute-start | bytes 294920 | tf_op jit(solution)/shard_map/ppermute | solution.py:272
  84.1 3.5 %collective-permute-start.7 = (bf16[128,256]{1,0:T(8,128)(2,1)S(1)}, bf16[128,256]{1,0:T(8,128)(2,1)S(1)}, u32[]{:S(2)}, u32[]{:S(2)}) collective-permute-start(bf16[128,256]{1,0:T(8,128)(2,1)S(1)} %get-tuple-element.254), channel_id=1, source_target_pairs={{64,160},{65,161},{66,162},{67,163},{68,164},{69,165},{70,166},{71... | collective-permute-start | bytes 196616 | tf_op jit(solution)/shard_map/ppermute | solution.py:272
  84.8 2.8 collective-permute-start.8
  85.5 2.1 collective-permute-start.9
  88.9 2.7 collective-permute-start.11
  89.6 2.0 collective-permute-start.12
  92.1 2.8 collective-permute-start.18
  92.7 2.0 collective-permute-start.15
  95.2 2.7 collective-permute-start.19
  95.9 2.0 collective-permute-start.20
  98.3 2.9 collective-permute-start.26
  99.0 2.2 collective-permute-start.23
  99.7 1.6 collective-permute-start.24
  101.6 174.2 %collective-permute-start.27 = (bf16[128,384]{1,0:T(8,128)(2,1)S(1)}, bf16[128,384]{1,0:T(8,128)(2,1)S(1)}, u32[]{:S(2)}, u32[]{:S(2)}) collective-permute-start(bf16[128,384]{1,0:T(8,128)(2,1)S(1)} %get-tuple-element.296), channel_id=1, source_target_pairs={{384,448},{385,449},{386,450},{387,451},{388,452},{389,453},{390,4... | collective-permute-start | bytes 294920 | tf_op jit(solution)/shard_map/ppermute | solution.py:272
  102.9 171.2 %collective-permute-start.28 = (bf16[128,256]{1,0:T(8,128)(2,1)S(1)}, bf16[128,256]{1,0:T(8,128)(2,1)S(1)}, u32[]{:S(2)}, u32[]{:S(2)}) collective-permute-start(bf16[128,256]{1,0:T(8,128)(2,1)S(1)} %get-tuple-element.297), channel_id=1, source_target_pairs={{384,480},{385,481},{386,482},{387,483},{388,484},{389,485},{390,4... | collective-permute-start | bytes 196616 | tf_op jit(solution)/shard_map/ppermute | solution.py:272
  104.2 171.6 %collective-permute-start.29 = (bf16[128,256]{1,0:T(8,128)(2,1)S(1)}, bf16[128,256]{1,0:T(8,128)(2,1)S(1)}, u32[]{:S(2)}, u32[]{:S(2)}) collective-permute-start(bf16[128,256]{1,0:T(8,128)(2,1)S(1)} %get-tuple-element.298), channel_id=1, source_target_pairs={{384,464},{385,465},{386,466},{387,467},{388,468},{389,469},{390,4... | collective-permute-start | bytes 196616 | tf_op jit(solution)/shard_map/ppermute | solution.py:272
  105.5 170.3 %collective-permute-start.30 = (bf16[128,256]{1,0:T(8,128)(2,1)S(1)}, bf16[128,256]{1,0:T(8,128)(2,1)S(1)}, u32[]{:S(2)}, u32[]{:S(2)}) collective-permute-start(bf16[128,256]{1,0:T(8,128)(2,1)S(1)} %get-tuple-element.299), channel_id=1, source_target_pairs={{384,496},{385,497},{386,498},{387,499},{388,500},{389,501},{390,5... | collective-permute-start | bytes 196616 | tf_op jit(solution)/shard_map/ppermute | solution.py:272
  (18 other events, 135.3 us)
